TPU v7x, 32 devices: a whole 2x2x4 slice. The times are simulated.
32 devices in a mesh: seq: 8 (over z, core), fsdp: 4 (over y, x).
Axes of the slice: x: 2, y: 2, z: 4, core: 2. Of those that a mesh axis runs over, the one named last changes fastest.
Arguments:
- hidden: bfloat16 [4, 2048, 3584], P('fsdp', 'seq'), may hold values from -6 to 6
- queries: bfloat16 [4, 2048, 2048], P('fsdp', 'seq'), may hold values from -6 to 6
- norm_gain: float32 [3584], replicated, may hold values from 0.1 to 1.9
- key_weight: bfloat16 [3584, 1024], P('fsdp'), may hold values from -0.09375 to 0.09375
- value_weight: bfloat16 [3584, 1024], P('fsdp'), may hold values from -0.09375 to 0.09375
- lengths: int32 [4], P('fsdp'), may hold values from 128 to 2048, as said below
Outputs:
- attended: bfloat16 [4, 2048, 2048], P('fsdp', 'seq')
Inputs may be any that keep to these rules, and one draw needn't show every extreme that they name: `lengths`: each length is a multiple of 128; in every draw some request fills all 2048 slots.
All inputs are finite; a program needn't handle non-finite values.
Results may differ from a plain program's by a relative error of at most 0.0082.
Values may be sent and summed in bfloat16 or wider, within the bound.
No kernel may reach another device: no remote copies, remote signals or barrier semaphores. Data moves between devices by JAX's collectives and lax.ppermute only.
A program may use at most 128 MiB of HBM per device.

v0:
```python
import jax
import jax.numpy as jnp
from jax import lax
from jax.sharding import PartitionSpec as P

HQ = 8
HK = 4
HD = 256
WINDOW = 4096


EPSILON = 1e-06
SOFTCAP = 50.0


def rotate(vectors, positions):
    halfway = vectors.shape[-1] // 2
    exponent = jnp.arange(halfway, dtype=jnp.float32) * (2.0 / vectors.shape[-1])
    frequency = jnp.exp(-jnp.log(10000.0) * exponent)
    angles = positions[:, None] * frequency[None, :]
    cosine = jnp.cos(angles)[:, None, :]
    sine = jnp.sin(angles)[:, None, :]
    first_half = vectors[..., :halfway]
    second_half = vectors[..., halfway:]
    return jnp.concatenate(
        [first_half * cosine - second_half * sine, second_half * cosine + first_half * sine],
        axis=-1,
    )


def attend(query_rows, key_rows, value_rows, query_pos, length):
    key_pos = jnp.arange(key_rows.shape[0], dtype=jnp.int32)
    scores = jnp.einsum("qgjd,kgd->gjqk", query_rows, key_rows, preferred_element_type=jnp.float32)
    scores = scores * (1.0 / jnp.sqrt(jnp.float32(query_rows.shape[-1])))
    capped = SOFTCAP * jnp.tanh(scores / SOFTCAP)
    visible = (key_pos[None, :] <= query_pos[:, None]) & (
        query_pos[:, None] - key_pos[None, :] < WINDOW
    )
    visible = visible & (key_pos[None, :] < length) & (key_pos[None, :] >= 0)
    weights = jnp.where(visible[None, None], jnp.exp(capped), 0.0)
    denominator = jnp.sum(weights, axis=-1)
    numerator = jnp.einsum(
        "gjqk,kgd->qgjd",
        weights.astype(jnp.bfloat16),
        value_rows,
        preferred_element_type=jnp.float32,
    )
    return (numerator, denominator)


def local(hidden, queries, norm_gain, key_weight, value_weight, lengths):
    row_count = hidden.shape[1]
    floats = hidden[0].astype(jnp.float32)
    factor = lax.rsqrt(jnp.mean(floats * floats, axis=-1, keepdims=True) + EPSILON)
    normed = (floats * factor * norm_gain).astype(jnp.bfloat16)
    pieces = (
        lax.all_gather(key_weight, "fsdp", axis=0, tiled=True),
        lax.all_gather(value_weight, "fsdp", axis=0, tiled=True),
    )
    key_proj = jnp.dot(normed, pieces[0], preferred_element_type=jnp.float32)
    value_proj = jnp.dot(normed, pieces[1], preferred_element_type=jnp.float32)
    first_row = lax.axis_index("seq") * row_count
    query_pos = first_row + jnp.arange(row_count, dtype=jnp.int32)
    positions = query_pos.astype(jnp.float32)
    key_heads = rotate(key_proj.reshape(row_count, HK, HD), positions).astype(jnp.bfloat16)
    value_heads = value_proj.astype(jnp.bfloat16).reshape(row_count, HK, HD)
    query_heads = rotate(queries[0].astype(jnp.float32).reshape(row_count, HQ, HD), positions)
    query_heads = query_heads.astype(jnp.bfloat16).reshape(row_count, HK, HQ // HK, HD)
    length = lengths[0]
    pieces = (
        lax.all_gather(key_heads, "seq", axis=0, tiled=True),
        lax.all_gather(value_heads, "seq", axis=0, tiled=True),
    )
    numerator, denominator = attend(query_heads, pieces[0], pieces[1], query_pos, length)
    valid = query_pos < length
    safe_total = jnp.where(valid[None, None, :], denominator, 1.0)
    result = numerator / jnp.transpose(safe_total, (2, 0, 1))[..., None]
    result = jnp.where(valid[:, None, None, None], result, 0.0).astype(jnp.bfloat16)
    return result.reshape(1, row_count, HQ * HD)


def solution(mesh):
    in_specs = (
        P("fsdp", "seq", None),
        P("fsdp", "seq", None),
        P(),
        P("fsdp", None),
        P("fsdp", None),
        P("fsdp"),
    )
    out_specs = P("fsdp", "seq", None)
    return jax.shard_map(local, mesh=mesh, in_specs=in_specs, out_specs=out_specs, check_vma=False)
```

profile of v0, /device:TPU:0, one launch (start us, length us, event | category | flops | bytes accessed | tf_op | source)
XLA Modules:
  0.0 286.5 jit_solution(7467075505360187766)
XLA Ops:
  6.5 0.7 all-gather.9.cloned.1.call-update
  7.3 0.7 all-gather.5.cloned.1.call-update
  8.1 0.4 fusion.10
  8.5 0.5 multiply_cosine_fusion
  9.1 81.6 %all-gather.9.cloned.1.call-done = bf16[3584,1024]{1,0:T(8,128)(2,1)} async-done(((bf16[896,1024]{1,0:T(8,128)(2,1)}), bf16[3584,1024]{1,0:T(8,128)(2,1)}) %all-gather.9.cloned.1.call-update) | async-done | bytes 7340048 | tf_op jit(solution)/shard_map/all_gather | solution.py:57
  90.7 10.1 %copy.8 = bf16[1024,3584]{1,0:T(8,128)(2,1)} copy(bf16[1024,3584]{0,1:T(8,128)(2,1)} %bitcast.66) | data formatting | bytes 14680064 | tf_op jit(solution)/shard_map/dot_general | solution.py:60
  100.8 6.1 %fusion.20 = f32[256,4,256]{0,2,1:T(8,128)S(1)} fusion(bf16[4,256,3584]{2,1,0:T(8,128)(2,1)} %bitcast.67, bf16[1,256,3584]{2,1,0:T(8,128)(2,1)S(1)} %copy-done, f32[3584]{0:T(1024)S(1)} %copy-done.2, f32[256]{0:T(256)S(1)} %add_rsqrt_fusion), kind=kOutput, calls=%fused_computation.25 | convolution fusion | flops 1882718208 | bytes 10238976 | tf_op jit(solution)/shard_map/dot_general | solution.py:60
  106.9 0.1 subtract_convert_fusion.1
  107.1 0.8 pad_maximum_fusion
  107.9 0.2 all-gather.7.cloned.1.call-start
  108.2 63.1 %all-gather.5.cloned.1.call-done = bf16[3584,1024]{1,0:T(8,128)(2,1)} async-done(((bf16[896,1024]{1,0:T(8,128)(2,1)}), bf16[3584,1024]{1,0:T(8,128)(2,1)}) %all-gather.5.cloned.1.call-update) | async-done | bytes 7340048 | tf_op jit(solution)/shard_map/all_gather | solution.py:58
  171.3 6.0 %fusion.32 = bf16[256,1024]{1,0:T(8,128)(2,1)} fusion(bf16[3584,1024]{1,0:T(8,128)(2,1)} %all-gather.5.cloned.1.call-done, bf16[1,256,3584]{2,1,0:T(8,128)(2,1)S(1)} %copy-done, f32[3584]{0:T(1024)S(1)} %copy-done.2, f32[256]{0:T(256)S(1)} %add_rsqrt_fusion), kind=kOutput, calls=%fused_computation.31 | convolution fusion | flops 1882980352 | bytes 9714688 | tf_op jit(solution)/shard_map/dot_general | solution.py:61
  177.3 2.1 copy.19
  179.4 0.1 copy.10
  179.5 0.1 copy.12
  179.6 0.2 copy.24
  180.5 0.1 fusion.44
  180.7 0.4 subtract_convert_fusion
  181.1 0.7 fusion.18
  181.8 38.9 %all-gather.11.cloned.1.call-done = bf16[2048,4,256]{0,2,1:T(8,128)(2,1)} async-done(((bf16[256,4,256]{0,2,1:T(8,128)(2,1)}), bf16[2048,4,256]{0,2,1:T(8,128)(2,1)}) %all-gather.11.cloned.1.call-update) | async-done | bytes 4194320 | tf_op jit(solution)/shard_map/all_gather | solution.py:71
  220.8 12.0 %fusion = (f32[4,2,256]{2,1,0:T(2,128)S(1)}, f32[4,2048,256,2]{2,1,3,0:T(8,128)}) fusion(pred[256,2048]{0,1:T(8,128)(4,1)S(1)} %fusion.18, bf16[256,4,2,128]{3,0,2,1:T(8,128)(2,1)S(1)} %bitcast.72, bf16[256,4,2,128]{3,0,2,1:T(8,128)(2,1)S(1)} %bitcast.71, bf16[2048,4,256]{0,2,1:T(8,128)(2,1)} %all-gather.11.cloned.1.call-done), kind=kOutput, calls=%fused_computation.1 | convolution fusion | flops 2166355968 | bytes 22552576 | tf_op jit(solution)/shard_map/qgjd,kgd->gjqk/dot_general | solution.py:33
  232.7 35.5 %all-gather.7.cloned.1.call-done = bf16[2048,4,256]{0,2,1:T(8,128)(2,1)} async-done(((bf16[256,4,256]{0,2,1:T(8,128)(2,1)}), bf16[2048,4,256]{0,2,1:T(8,128)(2,1)}) %all-gather.7.cloned.1.call-update) | async-done | bytes 4194320 | tf_op jit(solution)/shard_map/all_gather | solution.py:72
  268.2 10.3 %fusion.16 = bf16[256,4,2,256]{0,3,2,1:T(8,128)(2,1)S(1)} fusion(f32[4,2048,256,2]{2,1,3,0:T(8,128)} %get-tuple-element.14, pred[256,2048]{0,1:T(8,128)(4,1)S(1)} %fusion.18, bf16[2048,4,256]{0,2,1:T(8,128)(2,1)} %all-gather.7.cloned.1.call-done, f32[256,4,2]{0,2,1:T(2,128)S(1)} %select_bitcast_fusion, pred[256]{0:T(512)(128)(4,1)S(1)} %fusion.39), kind=kOutput, calls=%fused_computation.19 | convolution fusion | flops 2165833728 | bytes 22552832 | tf_op jit(solution)/shard_map/gjqk,kgd->qgjd/dot_general | solution.py:42
  278.5 1.4 copy.15
  (18 shorter events, 0.2 us)
Async XLA Ops:
  6.5 1.6 copy-start
  6.5 84.2 %all-gather.9.cloned.1.call-start = ((), (), s32[]{:S(2)}) async-start(), calls=%async_computation.2 | async-start | bytes 9175040 | tf_op jit(solution)/shard_map/all_gather | solution.py:57
  7.3 164.1 %all-gather.5.cloned.1.call-start = ((), (), s32[]{:S(2)}) async-start(), calls=%async_computation | async-start | bytes 9175040 | tf_op jit(solution)/shard_map/all_gather | solution.py:58
  8.0 212.8 %all-gather.11.cloned.1.call-start = ((), (), s32[]{:S(2)}) async-start(), calls=%async_computation.3 | async-start | bytes 4718592 | tf_op jit(solution)/shard_map/all_gather | solution.py:71
  90.7 10.1 %copy-start.2 = (f32[3584]{0:T(1024)S(1)}, f32[3584]{0:T(1024)}, u32[]{:S(2)}) copy-start(f32[3584]{0:T(1024)} %param.8) | copy-start | bytes 43012
  107.9 71.7 %copy-start.1 = (bf16[1,256,2048]{2,1,0:T(8,128)(2,1)S(1)}, bf16[1,256,2048]{2,1,0:T(8,128)(2,1)}, u32[]{:S(2)}) copy-start(bf16[1,256,2048]{2,1,0:T(8,128)(2,1)} %param.7) | copy-start | bytes 3145732
  107.9 160.3 %all-gather.7.cloned.1.call-start = ((), (), s32[]{:S(2)}) async-start(), calls=%async_computation.1 | async-start | bytes 4718592 | tf_op jit(solution)/shard_map/all_gather | solution.py:72
Sparse Core Ops, SparseCore 0:
  9.2 81.4 all-gather.8
  92.5 78.7 all-gather.4
  172.9 47.8 all-gather.10
  222.2 45.9 all-gather.6
where the time goes:
time: 287 us
  waiting for transfers between devices  221 us (77%)
  matrix products  34.3 us (12%)
  local copies, waits for them, and re-layouts  14.2 us (5%)
  between operations  13.9 us (5%)
  other arithmetic  3.14 us (1%)
    all_gather x1, waiting for transfers between devices, local(): lax.all_gather(key_weight, 'fsdp', axis=0, tiled=True)  81.6 us
    all_gather x1, waiting for transfers between devices, local(): lax.all_gather(value_weight, 'fsdp', axis=0, tiled=True)  63.1 us
    all_gather x1, waiting for transfers between devices, local(): lax.all_gather(key_heads, 'seq', axis=0, tiled=True)  38.9 us
    all_gather x1, waiting for transfers between devices, local(): lax.all_gather(value_heads, 'seq', axis=0, tiled=True)  35.5 us
    dot_general x1, matrix products, attend(): jnp.einsum('qgjd,kgd->gjqk', query_rows, key_rows, preferred_element_type...  12 us
    dot_general x1, matrix products, attend(): jnp.einsum('gjqk,kgd->qgjd', weights.astype(jnp.bfloat16), value_rows, pr...  10.3 us
    dot_general x1, local copies, waits for them, and re-layouts, local(): key_proj = jnp.dot(normed, pieces[0], preferred_element_type=jnp.float32)  10.1 us
    dot_general x1, matrix products, local(): key_proj = jnp.dot(normed, pieces[0], preferred_element_type=jnp.float32)  6.09 us
  transfers between devices with their start and end apart: 4, of which 4 were waited for; matrix products, arithmetic and copies ran while one was open for 14% of the time, Pallas kernels for 0%

commit v1 on v0

v1 whole, which is shorter than its diff:
```python
import functools
import math

import jax
import jax.numpy as jnp
from jax import lax
from jax.experimental import pallas as pl
from jax.experimental.pallas import tpu as pltpu
from jax.sharding import PartitionSpec as P


HQ = 8
HK = 4
HD = 256
WINDOW = 4096

EPSILON = 1e-06
SOFTCAP = 50.0
CORES = 2
HEADS = HK // CORES
GROUP = HQ // HK
MIB = 1 << 20


VMEM = pl.BlockSpec(memory_space=pltpu.VMEM)
SMEM = pl.BlockSpec(memory_space=pltpu.SMEM)

KEY, VALUE = "key", "value"
CHUNKS = (
    (KEY, 0, HD, False),
    (VALUE, 0, HD, True),
    (KEY, HD, HD, True),
    (VALUE, HD, HD, True),
)
SPLIT = (1,)


def turn(x, cos, sin):
    a, b = x[:, : HD // 2], x[:, HD // 2 :]
    return jnp.concatenate([a * cos - b * sin, b * cos + a * sin], axis=-1)


def norm_kernel(hidden, gain, normed, lead):
    groups, rows, depth = normed.shape
    floats = hidden[...].astype(jnp.float32)
    factor = lax.rsqrt(jnp.mean(floats * floats, axis=-1, keepdims=True) + EPSILON)
    result = (floats * factor * gain[...]).astype(jnp.bfloat16)
    for g in range(groups):
        normed[g] = result[:, g * depth : (g + 1) * depth]
        lead[g] = result[: rows // 2, g * depth : (g + 1) * depth]


def rope_kernel(meta, q_own, q_other, cosine, sine, rotated):
    core = meta[0]
    rows = q_own.shape[0]
    scale = 1.0 / (math.sqrt(HD) * SOFTCAP)
    for ref, place in ((q_own, core), (q_other, 1 - core)):
        first = pl.multiple_of(place * rows, rows)
        near = pl.multiple_of(place * (rows // 2), rows // 2)
        away = pl.multiple_of(rows + place * (rows // 2), rows // 2)
        cos, sin = (
            jnp.concatenate([t[pl.ds(near, rows // 2), :], t[pl.ds(away, rows // 2), :]])
            for t in (cosine, sine)
        )
        for h in range(HEADS * GROUP):
            at = pl.multiple_of((core * HEADS * GROUP + h) * HD, HD)
            turned = turn(ref[:, pl.ds(at, HD)].astype(jnp.float32), cos, sin)
            rotated[h, pl.ds(first, rows), :] = (turned * scale).astype(jnp.bfloat16)


def merge_kernel(size, meta, own, other, merged):
    core = meta[0]
    rows = own.shape[1]
    for ref, place in ((own, core), (other, 1 - core)):
        for g in range(own.shape[0]):
            for n in range(rows // size):
                at = pl.multiple_of((n * CORES + place) * size, size)
                merged[g, pl.ds(at, size), :] = ref[g, n * size : (n + 1) * size, :]


def project_kernel(rope, sources, meta, cosine, sine, *refs):
    acts = refs[:sources]
    pieces = refs[sources:-sources]
    outs = refs[-sources:]

    def rows_of(ref):
        total = None
        for i, piece in enumerate(pieces):
            term = jnp.dot(ref[meta[3 + i]], piece[...], preferred_element_type=jnp.float32)
            total = term if total is None else total + term
        return total

    def ready(total, at):
        if rope:
            stretch = slice(at, at + total.shape[0])
            total = turn(total, cosine[stretch, :], sine[stretch, :])
        return total.astype(jnp.bfloat16)

    block = acts[0].shape[1]
    made = ready(rows_of(acts[0]), 0)
    if sources == 1:
        outs[0][...] = made
        return
    rows = block // CORES
    outs[0][...] = made[:rows]
    outs[1][:rows, :] = made[rows:]

    @pl.when(meta[1] > 0)
    def _():
        outs[1][rows:, :] = ready(rows_of(acts[1]), block)

    @pl.when(meta[1] == 0)
    def _():
        outs[1][rows:, :] = jnp.zeros((rows, outs[1].shape[1]), jnp.bfloat16)


def slice_kernel(meta, whole, out):
    out[...] = whole[...]


def cut(meta, weight, at, width):
    return pl.pallas_call(
        slice_kernel,
        out_shape=jax.ShapeDtypeStruct((weight.shape[0], width), weight.dtype),
        grid_spec=pltpu.PrefetchScalarGridSpec(
            num_scalar_prefetch=1,
            grid=(1,),
            in_specs=[
                pl.BlockSpec(
                    (weight.shape[0], width),
                    lambda i, meta: (0, meta[0] * (HEADS * HD // width) + at // width),
                )
            ],
            out_specs=pl.BlockSpec((weight.shape[0], width), lambda i, meta: (0, 0)),
        ),
        compiler_params=pltpu.CompilerParams(vmem_limit_bytes=4 * MIB),
    )(meta, weight)


def attend_kernel(window, first_head, stage, key_at, value_at, meta, rotated, *refs):
    outs = 2 if stage != "open" else 0
    carried = 2 if stage == "close" else 0
    total, mixture = refs[-2:]
    if outs:
        out_own, out_other = refs[-4:-2]
    chip, core, length = meta[1], meta[0], meta[2]
    heads, block = GROUP, rotated.shape[1]
    first = chip * block
    half = block // CORES
    quarter = half // 2
    if carried:
        total_in, mixture_in = refs[:2]
        total[...] = total_in[...]
        mixture[...] = mixture_in[...]
        refs = refs[2:]

    def stretch(step, part, masked):
        ref, row, _ = key_at[step, part]
        keys = refs[ref][row : row + half, :]
        value = []
        for ref, row, column, size in value_at[step, part]:
            value.append(refs[ref][row : row + half, column : column + size])
        value = value[0] if len(value) == 1 else jnp.concatenate(value, axis=-1)
        mask = None
        if masked:
            shape = (block, half)
            q = first + lax.broadcasted_iota(jnp.int32, shape, 0)
            r = lax.broadcasted_iota(jnp.int32, shape, 1)
            k = first - step * block + part * quarter + r + jnp.where(r >= quarter, half - quarter, 0)
            mask = (k <= q) & (k < length)
            if window is not None:
                mask = mask & (q - k < window)
        for h in range(heads):
            scores = lax.dot_general(
                rotated[first_head + h],
                keys,
                (((1,), (1,)), ((), ())),
                preferred_element_type=jnp.float32,
            )
            weights = jnp.exp2(jnp.tanh(scores) * (SOFTCAP * math.log2(math.e)))
            if masked:
                weights = jnp.where(mask, weights, 0.0)
            summed = jnp.sum(weights, axis=-1, keepdims=True)
            product = jnp.dot(weights.astype(jnp.bfloat16), value, preferred_element_type=jnp.float32)
            if (step, part) == (0, 0):
                total[h], mixture[h] = summed, product
            else:
                total[h] += summed
                mixture[h] += product

    def group(step, parts, masked):
        for part in parts:
            stretch(step, part, masked)

    for step in sorted({s for s, _ in key_at}):
        parts = [p for s, p in sorted(key_at) if s == step]
        if step == 0:
            group(0, parts, True)
            continue
        inside = first - step * block + block <= length
        if window is not None:
            inside = inside & ((step + 1) * block <= window)
        pl.when((chip >= step) & inside)(functools.partial(group, step, parts, False))
        pl.when((chip >= step) & jnp.logical_not(inside))(functools.partial(group, step, parts, True))

    if outs:
        for ref, place in ((out_own, core), (out_other, 1 - core)):
            at = pl.multiple_of(place * half, half)
            position = first + at + lax.broadcasted_iota(jnp.int32, (half, 1), 0)
            valid = position < length
            for h in range(heads):
                safe = jnp.where(valid, total[h, pl.ds(at, half), :], 1.0)
                result = mixture[h, pl.ds(at, half), :] / safe
                ref[:, h * HD : (h + 1) * HD] = jnp.where(valid, result, 0.0).astype(jnp.bfloat16)


def call(kernel, outs, operands, scratch=(), flops=0, transcendentals=0, limit=None, scalars=1):
    return pl.pallas_call(
        kernel,
        out_shape=outs,
        in_specs=[SMEM] * scalars + [VMEM] * (len(operands) - scalars),
        out_specs=jax.tree.map(lambda _: VMEM, outs),
        scratch_shapes=list(scratch),
        cost_estimate=pl.CostEstimate(
            flops=flops,
            transcendentals=transcendentals,
            bytes_accessed=sum(x.size * x.dtype.itemsize for x in operands),
        ),
        compiler_params=pltpu.CompilerParams(vmem_limit_bytes=limit),
    )(*operands)


def local(seq, fsdp, hidden, queries, norm_gain, key_weight, value_weight, lengths):
    bf16 = jnp.bfloat16
    f32 = jnp.float32
    _, rows, depth = hidden.shape
    chips = seq // CORES
    block = rows * CORES
    lead = rows // 2
    shard = lax.axis_index("seq")
    core, chip = shard % CORES, shard // CORES
    member = lax.axis_index("fsdp")
    relay = fsdp == 4

    swap = [(i, i ^ 1) for i in range(seq)]
    both = ("seq", "fsdp")

    def route(offsets):
        return [
            (i * fsdp + j, i * fsdp + (j ^ offsets[i % CORES]))
            for i in range(seq)
            for j in range(fsdp)
        ]

    def climb(step):
        return [(s, s + CORES) for s in range((step - 1) * CORES, seq - CORES)]

    if relay:
        groups = 4
        ids = [member, member ^ (1 + core), member ^ (2 - core), member ^ 3]
    else:
        groups = 1
        ids = [0]
    meta = jnp.stack([jnp.asarray(v, jnp.int32) for v in [core, chip, lengths[0]] + ids])

    pieces = []
    for i, (kind, at, width, _) in enumerate(CHUNKS):
        weight = key_weight if kind == KEY else value_weight
        if i == 0:
            own = lax.dynamic_slice_in_dim(weight, core * HEADS * HD + at, width, 1)
        else:
            own = cut(meta, weight, at, width)
        if relay:
            near = lax.ppermute(own, both, route((1, 2)))
            next_ = lax.ppermute(own, both, route((2, 1)))
            far = lax.ppermute(near, both, route((2, 1)))
            pieces.append((own, near, next_, far))
        else:
            pieces.append((lax.all_gather(own, "fsdp", axis=0, tiled=True),))

    normed, leading = call(
        norm_kernel,
        (
            jax.ShapeDtypeStruct((groups, rows, depth // groups), bf16),
            jax.ShapeDtypeStruct((groups, lead, depth // groups), bf16),
        ),
        (hidden[0], norm_gain[None, :]),
        flops=5 * rows * depth,
        limit=24 * MIB,
        scalars=0,
    )

    def merge(size, own, other):
        return call(
            functools.partial(merge_kernel, size),
            jax.ShapeDtypeStruct((own.shape[0], CORES * own.shape[1], own.shape[2]), bf16),
            (meta, own, other),
            flops=own.size,
            limit=16 * MIB,
        )

    acts = (merge(lead, normed, lax.ppermute(normed, "seq", swap)),)
    if any(shifted for *_, shifted in CHUNKS):
        risen = lax.ppermute(leading, "seq", climb(1))
        more = (merge(lead, risen, lax.ppermute(risen, "seq", swap)),)
    q_other = lax.ppermute(queries[0], "seq", swap)

    exponent = jnp.arange(HD // 2, dtype=f32) * (2.0 / HD)
    frequency = jnp.exp(-jnp.log(10000.0) * exponent)

    def tables(slots):
        angles = slots.astype(f32)[:, None] * frequency[None, :]
        return jnp.cos(angles), jnp.sin(angles)

    slots = chip * block + jnp.arange(block, dtype=jnp.int32)
    ordered = slots.reshape(CORES, 2, lead).swapaxes(0, 1).reshape(block)
    laid = tables(jnp.concatenate([ordered, ordered[:rows] - block]))

    rotated = call(
        rope_kernel,
        jax.ShapeDtypeStruct((HEADS * GROUP, block, HD), bf16),
        (meta, queries[0], q_other, *laid),
        flops=10 * block * HEADS * GROUP * HD,
        limit=12 * MIB,
    )

    climbed = []
    for i, (kind, at, width, shifted) in enumerate(CHUNKS):
        sources = acts + more if shifted else acts
        made = call(
            functools.partial(project_kernel, kind == KEY, len(sources)),
            [
                jax.ShapeDtypeStruct((n, width), bf16)
                for n in ((rows, block) if shifted else (block,))
            ],
            (meta, *laid, *sources, *pieces[i]),
            flops=2 * block * depth * width,
            limit=12 * MIB,
        )
        steps = [made]
        for step in range(1, chips):
            sent = made[-1] if step == 1 else steps[-1]
            if shifted and step == chips - 1:
                sent = sent[:rows]
            steps.append(lax.ppermute(sent, "seq", climb(step)))
        climbed.append(steps)

    def place(shifted, step, part):
        if not shifted:
            return (step, part * rows) if step else ((0, 0), part * rows)
        if step == 0:
            return (0, part), 0
        if part == 1:
            return step, 0
        return ((0, 1), rows) if step == 1 else (step - 1, rows)

    window = WINDOW if WINDOW < chips * block else None
    mine, theirs = [], []
    for j in range(HEADS):
        stretches = [(step, part) for step in range(chips) for part in range(2)]
        stages = [("whole", stretches)]
        if j in SPLIT:
            stages = [("open", stretches[:-1]), ("close", stretches[-1:])]
        state = ()
        for stage, todo in stages:
            arrays, numbers = [], {}

            def number(i, step):
                if (i, step) not in numbers:
                    numbers[i, step] = len(arrays)
                    arrays.append(climbed[i][0][step[1]] if isinstance(step, tuple) else climbed[i][step])
                return numbers[i, step]

            key_at, value_at = {}, {}
            for i, (kind, at, width, shifted) in enumerate(CHUNKS):
                lo, hi = max(at, j * HD), min(at + width, (j + 1) * HD)
                if lo >= hi:
                    continue
                for spot in todo:
                    step, row = place(shifted, *spot)
                    if kind == KEY:
                        key_at[spot] = (number(i, step), row, 0)
                    else:
                        value_at.setdefault(spot, []).append((lo, number(i, step), row, lo - at, hi - lo))
            value_at = {spot: tuple(v[1:] for v in sorted(parts)) for spot, parts in value_at.items()}
            scratch = (
                pltpu.VMEM((GROUP, block, 1), f32),
                pltpu.VMEM((GROUP, block, HD), f32),
            )
            carry = (
                jax.ShapeDtypeStruct((GROUP, block, 1), f32),
                jax.ShapeDtypeStruct((GROUP, block, HD), f32),
            )
            results = (jax.ShapeDtypeStruct((rows, GROUP * HD), bf16),) * 2
            state = call(
                functools.partial(attend_kernel, window, j * GROUP, stage, key_at, value_at),
                carry if stage == "open" else results,
                (meta, rotated, *state, *arrays),
                scratch=() if stage == "open" else scratch,
                flops=4 * GROUP * block * rows * len(todo) * HD,
                transcendentals=2 * GROUP * block * rows * len(todo),
                limit=16 * MIB,
            )
        mine.append(state[0])
        theirs.append(lax.ppermute(state[1], "seq", swap))
    low = [jnp.where(core == 0, a, b) for a, b in zip(mine, theirs)]
    high = [jnp.where(core == 0, b, a) for a, b in zip(mine, theirs)]
    return jnp.concatenate(low + high, axis=1)[None]


def solution(mesh):
    in_specs = (
        P("fsdp", "seq", None),
        P("fsdp", "seq", None),
        P(),
        P("fsdp", None),
        P("fsdp", None),
        P("fsdp"),
    )
    out_specs = P("fsdp", "seq", None)
    seq, fsdp = mesh.shape["seq"], mesh.shape["fsdp"]

    def body(*args):
        return local(seq, fsdp, *args)

    return jax.shard_map(body, mesh=mesh, in_specs=in_specs, out_specs=out_specs, check_vma=False)
```

time: 287 us -> 141 us (0.49)
  the two profiles are of different devices: /device:TPU:0 before, /device:TPU:25 now
where the time goes in v1:
time: 141 us; the launch traced here: 140 us
  waiting for transfers between devices  64.2 us (46%)
  starting transfers between devices  34.5 us (24%)
  Pallas kernels  31.5 us (22%)
  local copies, waits for them, and re-layouts  6.59 us (5%)
  other arithmetic  2.64 us (2%)
    ppermute x12, waiting for transfers between devices, local(): steps.append(lax.ppermute(sent, 'seq', climb(step)))  36.4 us
    pallas_call x11, Pallas kernels, call(): pl.pallas_call(kernel, out_shape=outs, in_specs=[SMEM] * scalars + [VMEM]...  29.7 us
    ppermute x12, starting transfers between devices, local(): steps.append(lax.ppermute(sent, 'seq', climb(step)))  15.8 us
    ppermute x4, waiting for transfers between devices, local(): near = lax.ppermute(own, both, route((1, 2)))  13.4 us
    ppermute x1, waiting for transfers between devices, local(): risen = lax.ppermute(leading, 'seq', climb(1))  6.6 us
    ppermute x4, waiting for transfers between devices, local(): far = lax.ppermute(near, both, route((2, 1)))  5.92 us
    ppermute x4, starting transfers between devices, local(): next_ = lax.ppermute(own, both, route((2, 1)))  5.8 us
    ppermute x4, starting transfers between devices, local(): far = lax.ppermute(near, both, route((2, 1)))  4.96 us
  transfers between devices with their start and end apart: 30, of which 17 were waited for; matrix products, arithmetic and copies ran while one was open for 2% of the time, Pallas kernels for 21%

profile of v1, /device:TPU:25, one launch (start us, length us, event | category | flops | bytes accessed | tf_op | source)
XLA Modules:
  0.0 140.4 jit_solution(14481502957679851969)
XLA Ops:
  2.4 2.6 %shard_map.65 = (bf16[4,256,896]{2,1,0:T(8,128)(2,1)}, bf16[4,128,896]{2,1,0:T(8,128)(2,1)}) custom-call(bf16[256,3584]{1,0:T(8,128)(2,1)S(1)} %bitcast.13, f32[1,3584]{1,0:T(1,128)S(1)} %broadcast_in_dim.8.gain), custom_call_target="tpu_custom_call" | custom-call | flops 4587520 | bytes 1849344 | tf_op jit(solution)/shard_map/pallas_call | solution.py:218
  12.3 6.8 %collective-permute-done.10.refs_3_ = bf16[896,256]{1,0:T(8,128)(2,1)} collective-permute-done((bf16[896,256]{1,0:T(8,128)(2,1)S(1)}, bf16[896,256]{1,0:T(8,128)(2,1)}, u32[]{:S(2)}, u32[]{:S(2)}) %collective-permute-start.10) | collective-permute-done | bytes 458784 | tf_op jit(solution)/shard_map/ppermute | solution.py:274
  19.1 2.2 %collective-permute-start.3 = (bf16[896,256]{1,0:T(8,128)(2,1)S(1)}, bf16[896,256]{1,0:T(8,128)(2,1)S(1)}, u32[]{:S(2)}, u32[]{:S(2)}) collective-permute-start(bf16[896,256]{1,0:T(8,128)(2,1)S(1)} %constant_dynamic-slice_fusion.refs_1_), channel_id=1, source_target_pairs={{0,2},{1,3},{2,0},{3,1},{4,5},{5,4},{6,7},{7,6},{8,10},{9,11},{10,... | collective-permute-start | bytes 1376264 | tf_op jit(solution)/shard_map/ppermute | solution.py:275
  23.2 6.6 %collective-permute-done.8.own = bf16[4,128,896]{2,1,0:T(8,128)(2,1)} collective-permute-done((bf16[4,128,896]{2,1,0:T(8,128)(2,1)}, bf16[4,128,896]{2,1,0:T(8,128)(2,1)}, u32[]{:S(2)}, u32[]{:S(2)}) %collective-permute-start.8) | collective-permute-done | bytes 917536 | tf_op jit(solution)/shard_map/ppermute | solution.py:304
  37.0 5.5 %collective-permute-done.17.refs_3_ = bf16[896,256]{1,0:T(8,128)(2,1)} collective-permute-done((bf16[896,256]{1,0:T(8,128)(2,1)S(1)}, bf16[896,256]{1,0:T(8,128)(2,1)}, u32[]{:S(2)}, u32[]{:S(2)}) %collective-permute-start.17) | collective-permute-done | bytes 458784 | tf_op jit(solution)/shard_map/ppermute | solution.py:274
  43.7 2.2 %collective-permute-done.12.refs_5_ = bf16[896,256]{1,0:T(8,128)(2,1)} collective-permute-done((bf16[896,256]{1,0:T(8,128)(2,1)}, bf16[896,256]{1,0:T(8,128)(2,1)}, u32[]{:S(2)}, u32[]{:S(2)}) %collective-permute-start.12) | collective-permute-done | bytes 458784 | tf_op jit(solution)/shard_map/ppermute | solution.py:276
  47.2 3.7 %collective-permute-done.4.refs_4_ = bf16[896,256]{1,0:T(8,128)(2,1)S(1)} collective-permute-done((bf16[896,256]{1,0:T(8,128)(2,1)}, bf16[896,256]{1,0:T(8,128)(2,1)S(1)}, u32[]{:S(2)}, u32[]{:S(2)}) %collective-permute-start.4) | collective-permute-done | bytes 458784 | tf_op jit(solution)/shard_map/ppermute | solution.py:276
  58.4 2.4 %shard_map.66.refs_0_ = bf16[4,512,896]{2,1,0:T(8,128)(2,1)S(1)} custom-call(s32[7]{0:T(128)S(1)} %stack.27.meta, bf16[4,256,896]{2,1,0:T(8,128)(2,1)} %get-tuple-element.19.own, bf16[4,256,896]{2,1,0:T(8,128)(2,1)} %collective-permute-done.1.other), custom_call_target="tpu_custom_call" | custom-call | flops 917504 | bytes 3670044 | tf_op jit(solution)/shard_map/pallas_call | solution.py:218
  60.8 2.3 %shard_map.67.refs_0_ = bf16[512,256]{1,0:T(8,128)(2,1)S(1)} custom-call(s32[7]{0:T(128)S(1)} %stack.27.meta, f32[768,128]{1,0:T(8,128)S(1)} %get-tuple-element.38.cosine, f32[768,128]{1,0:T(8,128)S(1)} %get-tuple-element.37.sine, bf16[4,512,896]{2,1,0:T(8,128)(2,1)S(1)} %shard_map.66.refs_0_, bf16[896,256]{1,0:T(8,128)(2,1)S(1)} %constant_dynamic-slice_fusion.refs_1_, ...), custom_call_target="tpu_custom_call" | custom-call | flops 939524096 | bytes 6291484 | tf_op jit(solution)/shard_map/pallas_call | solution.py:218
  63.1 3.2 %shard_map.70 = (bf16[256,256]{1,0:T(8,128)(2,1)S(1)}, bf16[512,256]{1,0:T(8,128)(2,1)S(1)}) custom-call(s32[7]{0:T(128)S(1)} %stack.27.meta, f32[768,128]{1,0:T(8,128)S(1)} %get-tuple-element.38.cosine, f32[768,128]{1,0:T(8,128)S(1)} %get-tuple-element.37.sine, bf16[4,512,896]{2,1,0:T(8,128)(2,1)S(1)} %shard_map.66.refs_0_, ...), custom_call_target="tpu_custom_call" | custom-call | flops 939524096 | bytes 8126492 | tf_op jit(solution)/shard_map/pallas_call | solution.py:218
  69.0 3.0 %shard_map.75 = (bf16[256,256]{1,0:T(8,128)(2,1)S(1)}, bf16[512,256]{1,0:T(8,128)(2,1)S(1)}) custom-call(s32[7]{0:T(128)S(1)} %stack.27.meta, f32[768,128]{1,0:T(8,128)S(1)} %get-tuple-element.38.cosine, f32[768,128]{1,0:T(8,128)S(1)} %get-tuple-element.37.sine, bf16[4,512,896]{2,1,0:T(8,128)(2,1)S(1)} %shard_map.66.refs_0_, ...), custom_call_target="tpu_custom_call" | custom-call | flops 939524096 | bytes 8126492 | tf_op jit(solution)/shard_map/pallas_call | solution.py:218
  73.4 3.0 %shard_map.73 = (bf16[256,256]{1,0:T(8,128)(2,1)S(1)}, bf16[512,256]{1,0:T(8,128)(2,1)S(1)}) custom-call(s32[7]{0:T(128)S(1)} %stack.27.meta, f32[768,128]{1,0:T(8,128)S(1)} %get-tuple-element.38.cosine, f32[768,128]{1,0:T(8,128)S(1)} %get-tuple-element.37.sine, bf16[4,512,896]{2,1,0:T(8,128)(2,1)S(1)} %shard_map.66.refs_0_, ...), custom_call_target="tpu_custom_call" | custom-call | flops 939524096 | bytes 8126492 | tf_op jit(solution)/shard_map/pallas_call | solution.py:218
  77.7 4.6 %collective-permute-done.5.refs_1_ = bf16[512,256]{1,0:T(8,128)(2,1)S(1)} collective-permute-done((bf16[512,256]{1,0:T(8,128)(2,1)S(1)}, bf16[512,256]{1,0:T(8,128)(2,1)S(1)}, u32[]{:S(2)}, u32[]{:S(2)}) %collective-permute-start.5) | collective-permute-done | bytes 262176 | tf_op jit(solution)/shard_map/ppermute | solution.py:345
  84.9 3.0 %collective-permute-done.25.refs_6_ = bf16[512,256]{1,0:T(8,128)(2,1)S(1)} collective-permute-done((bf16[512,256]{1,0:T(8,128)(2,1)S(1)}, bf16[512,256]{1,0:T(8,128)(2,1)S(1)}, u32[]{:S(2)}, u32[]{:S(2)}) %collective-permute-start.25) | collective-permute-done | bytes 262176 | tf_op jit(solution)/shard_map/ppermute | solution.py:345
  89.2 4.3 %collective-permute-done.20.refs_2_ = bf16[512,256]{1,0:T(8,128)(2,1)S(1)} collective-permute-done((bf16[512,256]{1,0:T(8,128)(2,1)S(1)}, bf16[512,256]{1,0:T(8,128)(2,1)S(1)}, u32[]{:S(2)}, u32[]{:S(2)}) %collective-permute-start.20) | collective-permute-done | bytes 262176 | tf_op jit(solution)/shard_map/ppermute | solution.py:345
  94.8 4.3 %collective-permute-done.6.refs_2_ = bf16[512,256]{1,0:T(8,128)(2,1)S(1)} collective-permute-done((bf16[512,256]{1,0:T(8,128)(2,1)S(1)}, bf16[512,256]{1,0:T(8,128)(2,1)S(1)}, u32[]{:S(2)}, u32[]{:S(2)}) %collective-permute-start.6) | collective-permute-done | bytes 262176 | tf_op jit(solution)/shard_map/ppermute | solution.py:345
  101.4 3.4 %collective-permute-done.14.refs_7_ = bf16[512,256]{1,0:T(8,128)(2,1)S(1)} collective-permute-done((bf16[512,256]{1,0:T(8,128)(2,1)S(1)}, bf16[512,256]{1,0:T(8,128)(2,1)S(1)}, u32[]{:S(2)}, u32[]{:S(2)}) %collective-permute-start.14) | collective-permute-done | bytes 262176 | tf_op jit(solution)/shard_map/ppermute | solution.py:345
  106.1 4.3 %collective-permute-done.26.refs_7_ = bf16[512,256]{1,0:T(8,128)(2,1)S(1)} collective-permute-done((bf16[512,256]{1,0:T(8,128)(2,1)S(1)}, bf16[512,256]{1,0:T(8,128)(2,1)S(1)}, u32[]{:S(2)}, u32[]{:S(2)}) %collective-permute-start.26) | collective-permute-done | bytes 262176 | tf_op jit(solution)/shard_map/ppermute | solution.py:345
  111.7 4.3 %collective-permute-done.21.refs_3_ = bf16[512,256]{1,0:T(8,128)(2,1)S(1)} collective-permute-done((bf16[512,256]{1,0:T(8,128)(2,1)S(1)}, bf16[512,256]{1,0:T(8,128)(2,1)S(1)}, u32[]{:S(2)}, u32[]{:S(2)}) %collective-permute-start.21) | collective-permute-done | bytes 262176 | tf_op jit(solution)/shard_map/ppermute | solution.py:345
  117.5 4.4 %shard_map.76 = (f32[2,512,1]{2,1,0:T(8,128)S(1)}, f32[2,512,256]{2,1,0:T(8,128)S(1)}) custom-call(s32[7]{0:T(128)S(1)} %stack.27.meta, bf16[4,512,256]{2,1,0:T(8,128)(2,1)S(1)} %shard_map.64.rotated, bf16[256,256]{1,0:T(8,128)(2,1)S(1)} %get-tuple-element.25.refs_0_, bf16[512,256]{1,0:T(8,128)(2,1)S(1)} %get-tuple-element.26.refs_1_, ...), custom_call_target="tpu_custom_call" | custom-call | flops 1879048192 | bytes 2883612 | tf_op jit(solution)/shard_map/pallas_call | solution.py:218
  121.9 5.3 %collective-permute-done.28.refs_3_ = bf16[256,256]{1,0:T(8,128)(2,1)S(1)} collective-permute-done((bf16[256,256]{1,0:T(8,128)(2,1)S(1)}, bf16[256,256]{1,0:T(8,128)(2,1)S(1)}, u32[]{:S(2)}, u32[]{:S(2)}) %collective-permute-start.28) | collective-permute-done | bytes 131104 | tf_op jit(solution)/shard_map/ppermute | solution.py:345
  127.3 2.8 %collective-permute-done.27.refs_2_ = bf16[256,256]{1,0:T(8,128)(2,1)S(1)} collective-permute-done((bf16[256,256]{1,0:T(8,128)(2,1)S(1)}, bf16[256,256]{1,0:T(8,128)(2,1)S(1)}, u32[]{:S(2)}, u32[]{:S(2)}) %collective-permute-start.27) | collective-permute-done | bytes 131104 | tf_op jit(solution)/shard_map/ppermute | solution.py:345
  130.1 1.6 %shard_map.77 = (bf16[256,512]{1,0:T(8,128)(2,1)S(1)}, bf16[256,512]{1,0:T(8,128)(2,1)S(1)}) custom-call(s32[7]{0:T(128)S(1)} %stack.27.meta, bf16[4,512,256]{2,1,0:T(8,128)(2,1)S(1)} %shard_map.64.rotated, f32[2,512,1]{2,1,0:T(8,128)S(1)} %get-tuple-element.29.refs_0_, f32[2,512,256]{2,1,0:T(8,128)S(1)} %get-tuple-element.30.refs_1_, ...), custom_call_target="tpu_custom_call" | custom-call | flops 268435456 | bytes 2363420 | tf_op jit(solution)/shard_map/pallas_call | solution.py:218
  132.7 4.9 %shard_map.71 = (bf16[256,512]{1,0:T(8,128)(2,1)S(1)}, bf16[256,512]{1,0:T(8,128)(2,1)S(1)}) custom-call(s32[7]{0:T(128)S(1)} %stack.27.meta, bf16[4,512,256]{2,1,0:T(8,128)(2,1)S(1)} %shard_map.64.rotated, bf16[512,256]{1,0:T(8,128)(2,1)S(1)} %shard_map.67.refs_0_, bf16[512,256]{1,0:T(8,128)(2,1)S(1)} %collective-permute-done.5.refs_1_, ...), custom_call_target="tpu_custom_call" | custom-call | flops 2147483648 | bytes 3145756 | tf_op jit(solution)/shard_map/pallas_call | solution.py:218
  (80 shorter events, 48.6 us)
Async XLA Ops:
  5.0 47.1 %collective-permute-start.1 = (bf16[4,256,896]{2,1,0:T(8,128)(2,1)}, bf16[4,256,896]{2,1,0:T(8,128)(2,1)}, u32[]{:S(2)}, u32[]{:S(2)}) collective-permute-start(bf16[4,256,896]{2,1,0:T(8,128)(2,1)} %get-tuple-element.19.own), channel_id=1, source_target_pairs={{0,4},{4,0},{8,12},{12,8},{16,20},{20,16},{24,28},{28,24},{1,5},{5... | collective-permute-start | bytes 5505032 | tf_op jit(solution)/shard_map/ppermute | solution.py:302
  5.6 24.1 %collective-permute-start.8 = (bf16[4,128,896]{2,1,0:T(8,128)(2,1)}, bf16[4,128,896]{2,1,0:T(8,128)(2,1)}, u32[]{:S(2)}, u32[]{:S(2)}) collective-permute-start(bf16[4,128,896]{2,1,0:T(8,128)(2,1)} %get-tuple-element.20), channel_id=1, source_target_pairs={{0,8},{4,12},{8,16},{12,20},{16,24},{20,28},{1,9},{5,13},{9,17},{1... | collective-permute-start | bytes 2752520 | tf_op jit(solution)/shard_map/ppermute | solution.py:304
  12.0 19.2 %collective-permute-start.2 = (bf16[896,256]{1,0:T(8,128)(2,1)S(1)}, bf16[896,256]{1,0:T(8,128)(2,1)}, u32[]{:S(2)}, u32[]{:S(2)}) collective-permute-start(bf16[896,256]{1,0:T(8,128)(2,1)S(1)} %constant_dynamic-slice_fusion.refs_1_), channel_id=1, source_target_pairs={{0,1},{1,0},{2,3},{3,2},{4,6},{5,7},{6,4},{7,5},{8,9},{9,8},{10,11... | collective-permute-start | bytes 1376264 | tf_op jit(solution)/shard_map/ppermute | solution.py:274
  19.1 13.5 %collective-permute-start.3 = (bf16[896,256]{1,0:T(8,128)(2,1)S(1)}, bf16[896,256]{1,0:T(8,128)(2,1)S(1)}, u32[]{:S(2)}, u32[]{:S(2)}) collective-permute-start(bf16[896,256]{1,0:T(8,128)(2,1)S(1)} %constant_dynamic-slice_fusion.refs_1_), channel_id=1, source_target_pairs={{0,2},{1,3},{2,0},{3,1},{4,5},{5,4},{6,7},{7,6},{8,10},{9,11},{10,... | collective-permute-start | bytes 1376264 | tf_op jit(solution)/shard_map/ppermute | solution.py:275
  22.3 13.5 %collective-permute-start.22 = (bf16[896,256]{1,0:T(8,128)(2,1)S(1)}, bf16[896,256]{1,0:T(8,128)(2,1)}, u32[]{:S(2)}, u32[]{:S(2)}) collective-permute-start(bf16[896,256]{1,0:T(8,128)(2,1)S(1)} %shard_map.74.refs_2_), channel_id=1, source_target_pairs={{0,1},{1,0},{2,3},{3,2},{4,6},{5,7},{6,4},{7,5},{8,9},{9,8},{10,11... | collective-permute-start | bytes 1376264 | tf_op jit(solution)/shard_map/ppermute | solution.py:274
  29.8 22.6 %collective-permute-start.9 = (bf16[4,128,896]{2,1,0:T(8,128)(2,1)}, bf16[4,128,896]{2,1,0:T(8,128)(2,1)S(1)}, u32[]{:S(2)}, u32[]{:S(2)}) collective-permute-start(bf16[4,128,896]{2,1,0:T(8,128)(2,1)} %collective-permute-done.8.own), channel_id=1, source_target_pairs={{0,4},{4,0},{8,12},{12,8},{16,20},{20,16},{24,28},{28,24},{1,5},{5... | collective-permute-start | bytes 2752520 | tf_op jit(solution)/shard_map/ppermute | solution.py:305
  35.8 15.1 %collective-permute-start.4 = (bf16[896,256]{1,0:T(8,128)(2,1)}, bf16[896,256]{1,0:T(8,128)(2,1)S(1)}, u32[]{:S(2)}, u32[]{:S(2)}) collective-permute-start(bf16[896,256]{1,0:T(8,128)(2,1)} %collective-permute-done.2.refs_2_), channel_id=1, source_target_pairs={{0,2},{1,3},{2,0},{3,1},{4,5},{5,4},{6,7},{7,6},{8,10},{9,11},{10,... | collective-permute-start | bytes 1376264 | tf_op jit(solution)/shard_map/ppermute | solution.py:276
  42.5 23.8 %collective-permute-start.23 = (bf16[896,256]{1,0:T(8,128)(2,1)S(1)}, bf16[896,256]{1,0:T(8,128)(2,1)S(1)}, u32[]{:S(2)}, u32[]{:S(2)}) collective-permute-start(bf16[896,256]{1,0:T(8,128)(2,1)S(1)} %shard_map.74.refs_2_), channel_id=1, source_target_pairs={{0,2},{1,3},{2,0},{3,1},{4,5},{5,4},{6,7},{7,6},{8,10},{9,11},{10,... | collective-permute-start | bytes 1376264 | tf_op jit(solution)/shard_map/ppermute | solution.py:275
  46.0 21.7 %collective-permute-start.24 = (bf16[896,256]{1,0:T(8,128)(2,1)}, bf16[896,256]{1,0:T(8,128)(2,1)S(1)}, u32[]{:S(2)}, u32[]{:S(2)}) collective-permute-start(bf16[896,256]{1,0:T(8,128)(2,1)} %collective-permute-done.22.refs_3_), channel_id=1, source_target_pairs={{0,2},{1,3},{2,0},{3,1},{4,5},{5,4},{6,7},{7,6},{8,10},{9,11},{10,... | collective-permute-start | bytes 1376264 | tf_op jit(solution)/shard_map/ppermute | solution.py:276
  50.9 21.1 %collective-permute-start.18 = (bf16[896,256]{1,0:T(8,128)(2,1)S(1)}, bf16[896,256]{1,0:T(8,128)(2,1)S(1)}, u32[]{:S(2)}, u32[]{:S(2)}) collective-permute-start(bf16[896,256]{1,0:T(8,128)(2,1)S(1)} %shard_map.72.refs_2_), channel_id=1, source_target_pairs={{0,2},{1,3},{2,0},{3,1},{4,5},{5,4},{6,7},{7,6},{8,10},{9,11},{10,... | collective-permute-start | bytes 1376264 | tf_op jit(solution)/shard_map/ppermute | solution.py:275
  52.1 48.4 %collective-permute-start = (bf16[256,2048]{1,0:T(8,128)(2,1)}, bf16[256,2048]{1,0:T(8,128)(2,1)S(1)}, u32[]{:S(2)}, u32[]{:S(2)}) collective-permute-start(bf16[256,2048]{1,0:T(8,128)(2,1)} %bitcast.14), channel_id=1, source_target_pairs={{0,4},{4,0},{8,12},{12,8},{16,20},{20,16},{24,28},{28,24},{1,5},{5... | collective-permute-start | bytes 3145736 | tf_op jit(solution)/shard_map/ppermute | solution.py:306
  53.3 20.2 %collective-permute-start.19 = (bf16[896,256]{1,0:T(8,128)(2,1)}, bf16[896,256]{1,0:T(8,128)(2,1)S(1)}, u32[]{:S(2)}, u32[]{:S(2)}) collective-permute-start(bf16[896,256]{1,0:T(8,128)(2,1)} %collective-permute-done.17.refs_3_), channel_id=1, source_target_pairs={{0,2},{1,3},{2,0},{3,1},{4,5},{5,4},{6,7},{7,6},{8,10},{9,11},{10,... | collective-permute-start | bytes 1376264 | tf_op jit(solution)/shard_map/ppermute | solution.py:276
  66.4 17.2 %collective-permute-start.13 = (bf16[512,256]{1,0:T(8,128)(2,1)S(1)}, bf16[512,256]{1,0:T(8,128)(2,1)S(1)}, u32[]{:S(2)}, u32[]{:S(2)}) collective-permute-start(bf16[512,256]{1,0:T(8,128)(2,1)S(1)} %get-tuple-element.22.refs_5_), channel_id=1, source_target_pairs={{0,8},{4,12},{8,16},{12,20},{16,24},{20,28},{1,9},{5,13},{9,17},{1... | collective-permute-start | bytes 786440 | tf_op jit(solution)/shard_map/ppermute | solution.py:345
  67.7 14.6 %collective-permute-start.5 = (bf16[512,256]{1,0:T(8,128)(2,1)S(1)}, bf16[512,256]{1,0:T(8,128)(2,1)S(1)}, u32[]{:S(2)}, u32[]{:S(2)}) collective-permute-start(bf16[512,256]{1,0:T(8,128)(2,1)S(1)} %shard_map.67.refs_0_), channel_id=1, source_target_pairs={{0,8},{4,12},{8,16},{12,20},{16,24},{20,28},{1,9},{5,13},{9,17},{1... | collective-permute-start | bytes 786440 | tf_op jit(solution)/shard_map/ppermute | solution.py:345
  72.0 15.9 %collective-permute-start.25 = (bf16[512,256]{1,0:T(8,128)(2,1)S(1)}, bf16[512,256]{1,0:T(8,128)(2,1)S(1)}, u32[]{:S(2)}, u32[]{:S(2)}) collective-permute-start(bf16[512,256]{1,0:T(8,128)(2,1)S(1)} %get-tuple-element.28.refs_5_), channel_id=1, source_target_pairs={{0,8},{4,12},{8,16},{12,20},{16,24},{20,28},{1,9},{5,13},{9,17},{1... | collective-permute-start | bytes 786440 | tf_op jit(solution)/shard_map/ppermute | solution.py:345
  76.4 17.1 %collective-permute-start.20 = (bf16[512,256]{1,0:T(8,128)(2,1)S(1)}, bf16[512,256]{1,0:T(8,128)(2,1)S(1)}, u32[]{:S(2)}, u32[]{:S(2)}) collective-permute-start(bf16[512,256]{1,0:T(8,128)(2,1)S(1)} %get-tuple-element.26.refs_1_), channel_id=1, source_target_pairs={{0,8},{4,12},{8,16},{12,20},{16,24},{20,28},{1,9},{5,13},{9,17},{1... | collective-permute-start | bytes 786440 | tf_op jit(solution)/shard_map/ppermute | solution.py:345
  82.3 16.9 %collective-permute-start.6 = (bf16[512,256]{1,0:T(8,128)(2,1)S(1)}, bf16[512,256]{1,0:T(8,128)(2,1)S(1)}, u32[]{:S(2)}, u32[]{:S(2)}) collective-permute-start(bf16[512,256]{1,0:T(8,128)(2,1)S(1)} %collective-permute-done.5.refs_1_), channel_id=1, source_target_pairs={{8,16},{12,20},{16,24},{20,28},{9,17},{13,21},{17,25},{21,29},{10,... | collective-permute-start | bytes 786440 | tf_op jit(solution)/shard_map/ppermute | solution.py:345
  83.6 21.2 %collective-permute-start.14 = (bf16[512,256]{1,0:T(8,128)(2,1)S(1)}, bf16[512,256]{1,0:T(8,128)(2,1)S(1)}, u32[]{:S(2)}, u32[]{:S(2)}) collective-permute-start(bf16[512,256]{1,0:T(8,128)(2,1)S(1)} %collective-permute-done.13.refs_6_), channel_id=1, source_target_pairs={{8,16},{12,20},{16,24},{20,28},{9,17},{13,21},{17,25},{21,29},{10,... | collective-permute-start | bytes 786440 | tf_op jit(solution)/shard_map/ppermute | solution.py:345
  87.9 22.5 %collective-permute-start.26 = (bf16[512,256]{1,0:T(8,128)(2,1)S(1)}, bf16[512,256]{1,0:T(8,128)(2,1)S(1)}, u32[]{:S(2)}, u32[]{:S(2)}) collective-permute-start(bf16[512,256]{1,0:T(8,128)(2,1)S(1)} %collective-permute-done.25.refs_6_), channel_id=1, source_target_pairs={{8,16},{12,20},{16,24},{20,28},{9,17},{13,21},{17,25},{21,29},{10,... | collective-permute-start | bytes 786440 | tf_op jit(solution)/shard_map/ppermute | solution.py:345
  93.6 22.5 %collective-permute-start.21 = (bf16[512,256]{1,0:T(8,128)(2,1)S(1)}, bf16[512,256]{1,0:T(8,128)(2,1)S(1)}, u32[]{:S(2)}, u32[]{:S(2)}) collective-permute-start(bf16[512,256]{1,0:T(8,128)(2,1)S(1)} %collective-permute-done.20.refs_2_), channel_id=1, source_target_pairs={{8,16},{12,20},{16,24},{20,28},{9,17},{13,21},{17,25},{21,29},{10,... | collective-permute-start | bytes 786440 | tf_op jit(solution)/shard_map/ppermute | solution.py:345
  99.2 33.5 %collective-permute-start.7 = (bf16[512,256]{1,0:T(8,128)(2,1)S(1)}, bf16[512,256]{1,0:T(8,128)(2,1)S(1)}, u32[]{:S(2)}, u32[]{:S(2)}) collective-permute-start(bf16[512,256]{1,0:T(8,128)(2,1)S(1)} %collective-permute-done.6.refs_2_), channel_id=1, source_target_pairs={{16,24},{20,28},{17,25},{21,29},{18,26},{22,30},{19,27},{23,31}} | collective-permute-start | bytes 786440 | tf_op jit(solution)/shard_map/ppermute | solution.py:345
  104.8 27.9 %collective-permute-start.15 = (bf16[256,256]{1,0:T(8,128)(2,1)S(1)}, bf16[256,256]{1,0:T(8,128)(2,1)S(1)}, u32[]{:S(2)}, u32[]{:S(2)}) collective-permute-start(bf16[256,256]{1,0:T(8,128)(2,1)S(1)} %slice.18), channel_id=1, source_target_pairs={{16,24},{20,28},{17,25},{21,29},{18,26},{22,30},{19,27},{23,31}} | collective-permute-start | bytes 393224 | tf_op jit(solution)/shard_map/ppermute | solution.py:345
  110.4 16.8 %collective-permute-start.28 = (bf16[256,256]{1,0:T(8,128)(2,1)S(1)}, bf16[256,256]{1,0:T(8,128)(2,1)S(1)}, u32[]{:S(2)}, u32[]{:S(2)}) collective-permute-start(bf16[256,256]{1,0:T(8,128)(2,1)S(1)} %slice.20), channel_id=1, source_target_pairs={{16,24},{20,28},{17,25},{21,29},{18,26},{22,30},{19,27},{23,31}} | collective-permute-start | bytes 393224 | tf_op jit(solution)/shard_map/ppermute | solution.py:345
  116.0 14.0 %collective-permute-start.27 = (bf16[256,256]{1,0:T(8,128)(2,1)S(1)}, bf16[256,256]{1,0:T(8,128)(2,1)S(1)}, u32[]{:S(2)}, u32[]{:S(2)}) collective-permute-start(bf16[256,256]{1,0:T(8,128)(2,1)S(1)} %slice.19), channel_id=1, source_target_pairs={{16,24},{20,28},{17,25},{21,29},{18,26},{22,30},{19,27},{23,31}} | collective-permute-start | bytes 393224 | tf_op jit(solution)/shard_map/ppermute | solution.py:345
  (14 other events, 117.7 us)

commit v2 on v1

--- a/solution.py
+++ b/solution.py
@@ -24,8 +24,10 @@
 
 VMEM = pl.BlockSpec(memory_space=pltpu.VMEM)
 SMEM = pl.BlockSpec(memory_space=pltpu.SMEM)
+HBM = pl.BlockSpec(memory_space=pltpu.HBM)
 
 KEY, VALUE = "key", "value"
+HALF = HD // 2
 CHUNKS = (
     (KEY, 0, HD, False),
     (VALUE, 0, HD, True),
@@ -40,14 +42,40 @@
     return jnp.concatenate([a * cos - b * sin, b * cos + a * sin], axis=-1)
 
 
-def norm_kernel(hidden, gain, normed, lead):
+def normalize(rows, gain):
+    floats = rows.astype(jnp.float32)
+    factor = lax.rsqrt(jnp.mean(floats * floats, axis=-1, keepdims=True) + EPSILON)
+    return (floats * factor * gain).astype(jnp.bfloat16)
+
+
+def norm_kernel(gain, hidden, normed, held, sems):
     groups, rows, depth = normed.shape
-    floats = hidden[...].astype(jnp.float32)
-    factor = lax.rsqrt(jnp.mean(floats * floats, axis=-1, keepdims=True) + EPSILON)
-    result = (floats * factor * gain[...]).astype(jnp.bfloat16)
-    for g in range(groups):
-        normed[g] = result[:, g * depth : (g + 1) * depth]
-        lead[g] = result[: rows // 2, g * depth : (g + 1) * depth]
+    parts = sems.shape[0]
+    size = rows // parts
+    copies = [
+        pltpu.make_async_copy(hidden.at[n * size : (n + 1) * size, :], held.at[n], sems.at[n])
+        for n in range(parts)
+    ]
+    for copy in copies:
+        copy.start()
+    for n, copy in enumerate(copies):
+        copy.wait()
+        result = normalize(held[n], gain[...])
+        for g in range(groups):
+            normed[g, n * size : (n + 1) * size, :] = result[:, g * depth : (g + 1) * depth]
+
+
+def lead_kernel(meta, gain, own, other, merged):
+    groups, rows, depth = merged.shape
+    lead = rows // CORES
+
+    @pl.when(meta[1] > 0)
+    def _():
+        for ref, place in ((own, meta[0]), (other, 1 - meta[0])):
+            result = normalize(ref[...], gain[...])
+            for g in range(groups):
+                at = pl.multiple_of(place * lead, lead)
+                merged[g, pl.ds(at, lead), :] = result[:, g * depth : (g + 1) * depth]
 
 
 def rope_kernel(meta, q_own, q_other, cosine, sine, rotated):
@@ -114,25 +142,21 @@
         outs[1][rows:, :] = jnp.zeros((rows, outs[1].shape[1]), jnp.bfloat16)
 
 
-def slice_kernel(meta, whole, out):
-    out[...] = whole[...]
+def cut_kernel(at, meta, weight, out, sem):
+    width = out.shape[1]
+    first = pl.multiple_of(meta[0] * HEADS * HD + at, HALF)
+    copy = pltpu.make_async_copy(weight.at[:, pl.ds(first, width)], out, sem)
+    copy.start()
+    copy.wait()
 
 
 def cut(meta, weight, at, width):
     return pl.pallas_call(
-        slice_kernel,
+        functools.partial(cut_kernel, at),
         out_shape=jax.ShapeDtypeStruct((weight.shape[0], width), weight.dtype),
-        grid_spec=pltpu.PrefetchScalarGridSpec(
-            num_scalar_prefetch=1,
-            grid=(1,),
-            in_specs=[
-                pl.BlockSpec(
-                    (weight.shape[0], width),
-                    lambda i, meta: (0, meta[0] * (HEADS * HD // width) + at // width),
-                )
-            ],
-            out_specs=pl.BlockSpec((weight.shape[0], width), lambda i, meta: (0, 0)),
-        ),
+        in_specs=[SMEM, HBM],
+        out_specs=VMEM,
+        scratch_shapes=[pltpu.SemaphoreType.DMA],
         compiler_params=pltpu.CompilerParams(vmem_limit_bytes=4 * MIB),
     )(meta, weight)
 
@@ -278,31 +302,42 @@
         else:
             pieces.append((lax.all_gather(own, "fsdp", axis=0, tiled=True),))
 
-    normed, leading = call(
+    gain = norm_gain[None, :]
+    parts = 4
+    normed = pl.pallas_call(
         norm_kernel,
-        (
+        out_shape=jax.ShapeDtypeStruct((groups, rows, depth // groups), bf16),
+        in_specs=[VMEM, HBM],
+        out_specs=VMEM,
+        scratch_shapes=[
+            pltpu.VMEM((parts, rows // parts, depth), bf16),
+            pltpu.SemaphoreType.DMA((parts,)),
+        ],
+        cost_estimate=pl.CostEstimate(
+            flops=5 * rows * depth, transcendentals=0, bytes_accessed=4 * rows * depth
+        ),
+        compiler_params=pltpu.CompilerParams(vmem_limit_bytes=16 * MIB),
+    )(gain, hidden[0])
+    other = lax.ppermute(normed, "seq", swap)
+    merged = call(
+        functools.partial(merge_kernel, lead),
+        jax.ShapeDtypeStruct((groups, block, depth // groups), bf16),
+        (meta, normed, other),
+        flops=normed.size,
+        limit=16 * MIB,
+    )
+    acts = (merged,)
+    if any(shifted for *_, shifted in CHUNKS):
+        risen = lax.ppermute(hidden[0, :lead], "seq", climb(1))
+        across = lax.ppermute(risen, "seq", swap)
+        more = call(
+            lead_kernel,
             jax.ShapeDtypeStruct((groups, rows, depth // groups), bf16),
-            jax.ShapeDtypeStruct((groups, lead, depth // groups), bf16),
-        ),
-        (hidden[0], norm_gain[None, :]),
-        flops=5 * rows * depth,
-        limit=24 * MIB,
-        scalars=0,
-    )
-
-    def merge(size, own, other):
-        return call(
-            functools.partial(merge_kernel, size),
-            jax.ShapeDtypeStruct((own.shape[0], CORES * own.shape[1], own.shape[2]), bf16),
-            (meta, own, other),
-            flops=own.size,
+            (meta, gain, risen, across),
+            flops=5 * rows * depth,
             limit=16 * MIB,
         )
-
-    acts = (merge(lead, normed, lax.ppermute(normed, "seq", swap)),)
-    if any(shifted for *_, shifted in CHUNKS):
-        risen = lax.ppermute(leading, "seq", climb(1))
-        more = (merge(lead, risen, lax.ppermute(risen, "seq", swap)),)
+        more = (more,)
     q_other = lax.ppermute(queries[0], "seq", swap)
 
     exponent = jnp.arange(HD // 2, dtype=f32) * (2.0 / HD)

time: 141 us -> 143 us (1.014)
  Pallas kernels: 31.5 us -> 33.3 us
    pallas_call x3 -> x4, Pallas kernels: 1.81 us -> 5.08 us  [the longest x1 3.23 us: local(): pl.pallas_call(norm_kernel, out_shape=jax.ShapeDtypeStruct((groups, rows,...]
    pallas_call x11 -> x10, Pallas kernels: 29.7 us -> 28.2 us  [call(): pl.pallas_call(kernel, out_shape=outs, in_specs=[SMEM] * scalars + [VMEM]...]
  transfers between devices with their start and end apart: 30 -> 30, of which waited for: 17 -> 17; matrix products, arithmetic and copies ran while one was open for 2% -> 3% of each run, Pallas kernels for 21% -> 21%
where the time goes in v2:
time: 143 us; the launch traced here: 142 us
  waiting for transfers between devices  64.1 us (45%)
  starting transfers between devices  34.5 us (24%)
  Pallas kernels  33.3 us (23%)
  local copies, waits for them, and re-layouts  6.27 us (4%)
  other arithmetic  2.67 us (2%)
    ppermute x12, waiting for transfers between devices, local(): steps.append(lax.ppermute(sent, 'seq', climb(step)))  36.4 us
    pallas_call x10, Pallas kernels, call(): pl.pallas_call(kernel, out_shape=outs, in_specs=[SMEM] * scalars + [VMEM]...  28.2 us
    ppermute x12, starting transfers between devices, local(): steps.append(lax.ppermute(sent, 'seq', climb(step)))  15.8 us
    ppermute x4, waiting for transfers between devices, local(): near = lax.ppermute(own, both, route((1, 2)))  13.3 us
    ppermute x1, waiting for transfers between devices, local(): risen = lax.ppermute(hidden[0, :lead], 'seq', climb(1))  6.57 us
    ppermute x4, waiting for transfers between devices, local(): far = lax.ppermute(near, both, route((2, 1)))  5.93 us
    ppermute x4, starting transfers between devices, local(): next_ = lax.ppermute(own, both, route((2, 1)))  5.8 us
    ppermute x4, starting transfers between devices, local(): far = lax.ppermute(near, both, route((2, 1)))  4.94 us
  transfers between devices with their start and end apart: 30, of which 17 were waited for; matrix products, arithmetic and copies ran while one was open for 3% of the time, Pallas kernels for 21%

profile of v2, /device:TPU:25, one launch (start us, length us, event | category | flops | bytes accessed | tf_op | source)
XLA Modules:
  0.0 141.9 jit_solution(12999095635140001433)
XLA Ops:
  2.2 3.2 %shard_map.65.own = bf16[4,256,896]{2,1,0:T(8,128)(2,1)} custom-call(f32[1,3584]{1,0:T(1,128)S(1)} %broadcast_in_dim.8.gain, bf16[256,3584]{1,0:T(8,128)(2,1)S(1)} %bitcast.15), custom_call_target="tpu_custom_call" | custom-call | flops 4587520 | bytes 3670016 | tf_op jit(solution)/shard_map/pallas_call | solution.py:307
  13.9 6.7 %collective-permute-done.10.refs_3_ = bf16[896,256]{1,0:T(8,128)(2,1)} collective-permute-done((bf16[896,256]{1,0:T(8,128)(2,1)S(1)}, bf16[896,256]{1,0:T(8,128)(2,1)}, u32[]{:S(2)}, u32[]{:S(2)}) %collective-permute-start.10) | collective-permute-done | bytes 458784 | tf_op jit(solution)/shard_map/ppermute | solution.py:298
  20.6 2.2 %collective-permute-start.3 = (bf16[896,256]{1,0:T(8,128)(2,1)S(1)}, bf16[896,256]{1,0:T(8,128)(2,1)S(1)}, u32[]{:S(2)}, u32[]{:S(2)}) collective-permute-start(bf16[896,256]{1,0:T(8,128)(2,1)S(1)} %constant_dynamic-slice_fusion.refs_1_), channel_id=1, source_target_pairs={{0,2},{1,3},{2,0},{3,1},{4,5},{5,4},{6,7},{7,6},{8,10},{9,11},{10,... | collective-permute-start | bytes 1376264 | tf_op jit(solution)/shard_map/ppermute | solution.py:299
  24.7 6.6 %collective-permute-done.8.own = bf16[128,3584]{1,0:T(8,128)(2,1)} collective-permute-done((bf16[128,3584]{1,0:T(8,128)(2,1)}, bf16[128,3584]{1,0:T(8,128)(2,1)}, u32[]{:S(2)}, u32[]{:S(2)}) %collective-permute-start.8) | collective-permute-done | bytes 917536 | tf_op jit(solution)/shard_map/ppermute | solution.py:331
  38.6 5.5 %collective-permute-done.17.refs_3_ = bf16[896,256]{1,0:T(8,128)(2,1)} collective-permute-done((bf16[896,256]{1,0:T(8,128)(2,1)S(1)}, bf16[896,256]{1,0:T(8,128)(2,1)}, u32[]{:S(2)}, u32[]{:S(2)}) %collective-permute-start.17) | collective-permute-done | bytes 458784 | tf_op jit(solution)/shard_map/ppermute | solution.py:298
  45.3 2.2 %collective-permute-done.12.refs_5_ = bf16[896,256]{1,0:T(8,128)(2,1)} collective-permute-done((bf16[896,256]{1,0:T(8,128)(2,1)}, bf16[896,256]{1,0:T(8,128)(2,1)}, u32[]{:S(2)}, u32[]{:S(2)}) %collective-permute-start.12) | collective-permute-done | bytes 458784 | tf_op jit(solution)/shard_map/ppermute | solution.py:300
  48.8 3.7 %collective-permute-done.4.refs_4_ = bf16[896,256]{1,0:T(8,128)(2,1)S(1)} collective-permute-done((bf16[896,256]{1,0:T(8,128)(2,1)}, bf16[896,256]{1,0:T(8,128)(2,1)S(1)}, u32[]{:S(2)}, u32[]{:S(2)}) %collective-permute-start.4) | collective-permute-done | bytes 458784 | tf_op jit(solution)/shard_map/ppermute | solution.py:300
  57.5 2.4 %shard_map.66.refs_0_ = bf16[4,512,896]{2,1,0:T(8,128)(2,1)S(1)} custom-call(s32[7]{0:T(128)S(1)} %stack.27.meta, bf16[4,256,896]{2,1,0:T(8,128)(2,1)} %shard_map.65.own, bf16[4,256,896]{2,1,0:T(8,128)(2,1)} %collective-permute-done.1.other), custom_call_target="tpu_custom_call" | custom-call | flops 917504 | bytes 3670044 | tf_op jit(solution)/shard_map/pallas_call | solution.py:242
  59.9 2.2 %shard_map.68.refs_1_ = bf16[4,256,896]{2,1,0:T(8,128)(2,1)S(1)} custom-call(s32[7]{0:T(128)S(1)} %stack.27.meta, f32[1,3584]{1,0:T(1,128)S(1)} %broadcast_in_dim.8.gain, bf16[128,3584]{1,0:T(8,128)(2,1)} %collective-permute-done.8.own, bf16[128,3584]{1,0:T(8,128)(2,1)S(1)} %copy-done.5), custom_call_target="tpu_custom_call" | custom-call | flops 4587520 | bytes 1849372 | tf_op jit(solution)/shard_map/pallas_call | solution.py:242
  62.2 2.3 %shard_map.67.refs_0_ = bf16[512,256]{1,0:T(8,128)(2,1)S(1)} custom-call(s32[7]{0:T(128)S(1)} %stack.27.meta, f32[768,128]{1,0:T(8,128)S(1)} %get-tuple-element.34.cosine, f32[768,128]{1,0:T(8,128)S(1)} %get-tuple-element.33.sine, bf16[4,512,896]{2,1,0:T(8,128)(2,1)S(1)} %shard_map.66.refs_0_, bf16[896,256]{1,0:T(8,128)(2,1)S(1)} %constant_dynamic-slice_fusion.refs_1_, ...), custom_call_target="tpu_custom_call" | custom-call | flops 939524096 | bytes 6291484 | tf_op jit(solution)/shard_map/pallas_call | solution.py:242
  64.5 3.2 %shard_map.70 = (bf16[256,256]{1,0:T(8,128)(2,1)S(1)}, bf16[512,256]{1,0:T(8,128)(2,1)S(1)}) custom-call(s32[7]{0:T(128)S(1)} %stack.27.meta, f32[768,128]{1,0:T(8,128)S(1)} %get-tuple-element.34.cosine, f32[768,128]{1,0:T(8,128)S(1)} %get-tuple-element.33.sine, bf16[4,512,896]{2,1,0:T(8,128)(2,1)S(1)} %shard_map.66.refs_0_, ...), custom_call_target="tpu_custom_call" | custom-call | flops 939524096 | bytes 8126492 | tf_op jit(solution)/shard_map/pallas_call | solution.py:242
  70.3 3.0 %shard_map.75 = (bf16[256,256]{1,0:T(8,128)(2,1)S(1)}, bf16[512,256]{1,0:T(8,128)(2,1)S(1)}) custom-call(s32[7]{0:T(128)S(1)} %stack.27.meta, f32[768,128]{1,0:T(8,128)S(1)} %get-tuple-element.34.cosine, f32[768,128]{1,0:T(8,128)S(1)} %get-tuple-element.33.sine, bf16[4,512,896]{2,1,0:T(8,128)(2,1)S(1)} %shard_map.66.refs_0_, ...), custom_call_target="tpu_custom_call" | custom-call | flops 939524096 | bytes 8126492 | tf_op jit(solution)/shard_map/pallas_call | solution.py:242
  74.8 3.0 %shard_map.73 = (bf16[256,256]{1,0:T(8,128)(2,1)S(1)}, bf16[512,256]{1,0:T(8,128)(2,1)S(1)}) custom-call(s32[7]{0:T(128)S(1)} %stack.27.meta, f32[768,128]{1,0:T(8,128)S(1)} %get-tuple-element.34.cosine, f32[768,128]{1,0:T(8,128)S(1)} %get-tuple-element.33.sine, bf16[4,512,896]{2,1,0:T(8,128)(2,1)S(1)} %shard_map.66.refs_0_, ...), custom_call_target="tpu_custom_call" | custom-call | flops 939524096 | bytes 8126492 | tf_op jit(solution)/shard_map/pallas_call | solution.py:242
  79.1 4.6 %collective-permute-done.5.refs_1_ = bf16[512,256]{1,0:T(8,128)(2,1)S(1)} collective-permute-done((bf16[512,256]{1,0:T(8,128)(2,1)S(1)}, bf16[512,256]{1,0:T(8,128)(2,1)S(1)}, u32[]{:S(2)}, u32[]{:S(2)}) %collective-permute-start.5) | collective-permute-done | bytes 262176 | tf_op jit(solution)/shard_map/ppermute | solution.py:380
  86.3 3.0 %collective-permute-done.25.refs_6_ = bf16[512,256]{1,0:T(8,128)(2,1)S(1)} collective-permute-done((bf16[512,256]{1,0:T(8,128)(2,1)S(1)}, bf16[512,256]{1,0:T(8,128)(2,1)S(1)}, u32[]{:S(2)}, u32[]{:S(2)}) %collective-permute-start.25) | collective-permute-done | bytes 262176 | tf_op jit(solution)/shard_map/ppermute | solution.py:380
  90.6 4.3 %collective-permute-done.20.refs_2_ = bf16[512,256]{1,0:T(8,128)(2,1)S(1)} collective-permute-done((bf16[512,256]{1,0:T(8,128)(2,1)S(1)}, bf16[512,256]{1,0:T(8,128)(2,1)S(1)}, u32[]{:S(2)}, u32[]{:S(2)}) %collective-permute-start.20) | collective-permute-done | bytes 262176 | tf_op jit(solution)/shard_map/ppermute | solution.py:380
  96.2 4.3 %collective-permute-done.6.refs_2_ = bf16[512,256]{1,0:T(8,128)(2,1)S(1)} collective-permute-done((bf16[512,256]{1,0:T(8,128)(2,1)S(1)}, bf16[512,256]{1,0:T(8,128)(2,1)S(1)}, u32[]{:S(2)}, u32[]{:S(2)}) %collective-permute-start.6) | collective-permute-done | bytes 262176 | tf_op jit(solution)/shard_map/ppermute | solution.py:380
  102.8 3.4 %collective-permute-done.14.refs_7_ = bf16[512,256]{1,0:T(8,128)(2,1)S(1)} collective-permute-done((bf16[512,256]{1,0:T(8,128)(2,1)S(1)}, bf16[512,256]{1,0:T(8,128)(2,1)S(1)}, u32[]{:S(2)}, u32[]{:S(2)}) %collective-permute-start.14) | collective-permute-done | bytes 262176 | tf_op jit(solution)/shard_map/ppermute | solution.py:380
  107.4 4.3 %collective-permute-done.26.refs_7_ = bf16[512,256]{1,0:T(8,128)(2,1)S(1)} collective-permute-done((bf16[512,256]{1,0:T(8,128)(2,1)S(1)}, bf16[512,256]{1,0:T(8,128)(2,1)S(1)}, u32[]{:S(2)}, u32[]{:S(2)}) %collective-permute-start.26) | collective-permute-done | bytes 262176 | tf_op jit(solution)/shard_map/ppermute | solution.py:380
  113.2 4.1 %collective-permute-done.21.refs_3_ = bf16[512,256]{1,0:T(8,128)(2,1)S(1)} collective-permute-done((bf16[512,256]{1,0:T(8,128)(2,1)S(1)}, bf16[512,256]{1,0:T(8,128)(2,1)S(1)}, u32[]{:S(2)}, u32[]{:S(2)}) %collective-permute-start.21) | collective-permute-done | bytes 262176 | tf_op jit(solution)/shard_map/ppermute | solution.py:380
  118.7 4.4 %shard_map.76 = (f32[2,512,1]{2,1,0:T(8,128)S(1)}, f32[2,512,256]{2,1,0:T(8,128)S(1)}) custom-call(s32[7]{0:T(128)S(1)} %stack.27.meta, bf16[4,512,256]{2,1,0:T(8,128)(2,1)S(1)} %shard_map.64.rotated, bf16[256,256]{1,0:T(8,128)(2,1)S(1)} %get-tuple-element.21.refs_0_, bf16[512,256]{1,0:T(8,128)(2,1)S(1)} %get-tuple-element.22.refs_1_, ...), custom_call_target="tpu_custom_call" | custom-call | flops 1879048192 | bytes 2883612 | tf_op jit(solution)/shard_map/pallas_call | solution.py:242
  123.1 5.5 %collective-permute-done.28.refs_3_ = bf16[256,256]{1,0:T(8,128)(2,1)S(1)} collective-permute-done((bf16[256,256]{1,0:T(8,128)(2,1)S(1)}, bf16[256,256]{1,0:T(8,128)(2,1)S(1)}, u32[]{:S(2)}, u32[]{:S(2)}) %collective-permute-start.28) | collective-permute-done | bytes 131104 | tf_op jit(solution)/shard_map/ppermute | solution.py:380
  128.6 2.8 %collective-permute-done.27.refs_2_ = bf16[256,256]{1,0:T(8,128)(2,1)S(1)} collective-permute-done((bf16[256,256]{1,0:T(8,128)(2,1)S(1)}, bf16[256,256]{1,0:T(8,128)(2,1)S(1)}, u32[]{:S(2)}, u32[]{:S(2)}) %collective-permute-start.27) | collective-permute-done | bytes 131104 | tf_op jit(solution)/shard_map/ppermute | solution.py:380
  134.0 5.2 %shard_map.71 = (bf16[256,512]{1,0:T(8,128)(2,1)S(1)}, bf16[256,512]{1,0:T(8,128)(2,1)S(1)}) custom-call(s32[7]{0:T(128)S(1)} %stack.27.meta, bf16[4,512,256]{2,1,0:T(8,128)(2,1)S(1)} %shard_map.64.rotated, bf16[512,256]{1,0:T(8,128)(2,1)S(1)} %shard_map.67.refs_0_, bf16[512,256]{1,0:T(8,128)(2,1)S(1)} %collective-permute-done.5.refs_1_, ...), custom_call_target="tpu_custom_call" | custom-call | flops 2147483648 | bytes 3145756 | tf_op jit(solution)/shard_map/pallas_call | solution.py:242
  (81 shorter events, 48.6 us)
Async XLA Ops:
  5.5 48.2 %collective-permute-start.1 = (bf16[4,256,896]{2,1,0:T(8,128)(2,1)}, bf16[4,256,896]{2,1,0:T(8,128)(2,1)}, u32[]{:S(2)}, u32[]{:S(2)}) collective-permute-start(bf16[4,256,896]{2,1,0:T(8,128)(2,1)} %shard_map.65.own), channel_id=1, source_target_pairs={{0,4},{4,0},{8,12},{12,8},{16,20},{20,16},{24,28},{28,24},{1,5},{5... | collective-permute-start | bytes 5505032 | tf_op jit(solution)/shard_map/ppermute | solution.py:321
  7.2 24.1 %collective-permute-start.8 = (bf16[128,3584]{1,0:T(8,128)(2,1)}, bf16[128,3584]{1,0:T(8,128)(2,1)}, u32[]{:S(2)}, u32[]{:S(2)}) collective-permute-start(bf16[128,3584]{1,0:T(8,128)(2,1)} %slice_bitcast_fusion), channel_id=1, source_target_pairs={{0,8},{4,12},{8,16},{12,20},{16,24},{20,28},{1,9},{5,13},{9,17},{1... | collective-permute-start | bytes 2752520 | tf_op jit(solution)/shard_map/ppermute | solution.py:331
  13.6 19.2 %collective-permute-start.2 = (bf16[896,256]{1,0:T(8,128)(2,1)S(1)}, bf16[896,256]{1,0:T(8,128)(2,1)}, u32[]{:S(2)}, u32[]{:S(2)}) collective-permute-start(bf16[896,256]{1,0:T(8,128)(2,1)S(1)} %constant_dynamic-slice_fusion.refs_1_), channel_id=1, source_target_pairs={{0,1},{1,0},{2,3},{3,2},{4,6},{5,7},{6,4},{7,5},{8,9},{9,8},{10,11... | collective-permute-start | bytes 1376264 | tf_op jit(solution)/shard_map/ppermute | solution.py:298
  20.6 13.5 %collective-permute-start.3 = (bf16[896,256]{1,0:T(8,128)(2,1)S(1)}, bf16[896,256]{1,0:T(8,128)(2,1)S(1)}, u32[]{:S(2)}, u32[]{:S(2)}) collective-permute-start(bf16[896,256]{1,0:T(8,128)(2,1)S(1)} %constant_dynamic-slice_fusion.refs_1_), channel_id=1, source_target_pairs={{0,2},{1,3},{2,0},{3,1},{4,5},{5,4},{6,7},{7,6},{8,10},{9,11},{10,... | collective-permute-start | bytes 1376264 | tf_op jit(solution)/shard_map/ppermute | solution.py:299
  23.8 13.5 %collective-permute-start.22 = (bf16[896,256]{1,0:T(8,128)(2,1)S(1)}, bf16[896,256]{1,0:T(8,128)(2,1)}, u32[]{:S(2)}, u32[]{:S(2)}) collective-permute-start(bf16[896,256]{1,0:T(8,128)(2,1)S(1)} %shard_map.74.refs_2_), channel_id=1, source_target_pairs={{0,1},{1,0},{2,3},{3,2},{4,6},{5,7},{6,4},{7,5},{8,9},{9,8},{10,11... | collective-permute-start | bytes 1376264 | tf_op jit(solution)/shard_map/ppermute | solution.py:298
  31.3 22.6 %collective-permute-start.9 = (bf16[128,3584]{1,0:T(8,128)(2,1)}, bf16[128,3584]{1,0:T(8,128)(2,1)S(1)}, u32[]{:S(2)}, u32[]{:S(2)}) collective-permute-start(bf16[128,3584]{1,0:T(8,128)(2,1)} %collective-permute-done.8.own), channel_id=1, source_target_pairs={{0,4},{4,0},{8,12},{12,8},{16,20},{20,16},{24,28},{28,24},{1,5},{5... | collective-permute-start | bytes 2752520 | tf_op jit(solution)/shard_map/ppermute | solution.py:332
  37.3 15.1 %collective-permute-start.4 = (bf16[896,256]{1,0:T(8,128)(2,1)}, bf16[896,256]{1,0:T(8,128)(2,1)S(1)}, u32[]{:S(2)}, u32[]{:S(2)}) collective-permute-start(bf16[896,256]{1,0:T(8,128)(2,1)} %collective-permute-done.2.refs_2_), channel_id=1, source_target_pairs={{0,2},{1,3},{2,0},{3,1},{4,5},{5,4},{6,7},{7,6},{8,10},{9,11},{10,... | collective-permute-start | bytes 1376264 | tf_op jit(solution)/shard_map/ppermute | solution.py:300
  44.1 23.6 %collective-permute-start.23 = (bf16[896,256]{1,0:T(8,128)(2,1)S(1)}, bf16[896,256]{1,0:T(8,128)(2,1)S(1)}, u32[]{:S(2)}, u32[]{:S(2)}) collective-permute-start(bf16[896,256]{1,0:T(8,128)(2,1)S(1)} %shard_map.74.refs_2_), channel_id=1, source_target_pairs={{0,2},{1,3},{2,0},{3,1},{4,5},{5,4},{6,7},{7,6},{8,10},{9,11},{10,... | collective-permute-start | bytes 1376264 | tf_op jit(solution)/shard_map/ppermute | solution.py:299
  47.5 21.5 %collective-permute-start.24 = (bf16[896,256]{1,0:T(8,128)(2,1)}, bf16[896,256]{1,0:T(8,128)(2,1)S(1)}, u32[]{:S(2)}, u32[]{:S(2)}) collective-permute-start(bf16[896,256]{1,0:T(8,128)(2,1)} %collective-permute-done.22.refs_3_), channel_id=1, source_target_pairs={{0,2},{1,3},{2,0},{3,1},{4,5},{5,4},{6,7},{7,6},{8,10},{9,11},{10,... | collective-permute-start | bytes 1376264 | tf_op jit(solution)/shard_map/ppermute | solution.py:300
  52.4 20.9 %collective-permute-start.18 = (bf16[896,256]{1,0:T(8,128)(2,1)S(1)}, bf16[896,256]{1,0:T(8,128)(2,1)S(1)}, u32[]{:S(2)}, u32[]{:S(2)}) collective-permute-start(bf16[896,256]{1,0:T(8,128)(2,1)S(1)} %shard_map.72.refs_2_), channel_id=1, source_target_pairs={{0,2},{1,3},{2,0},{3,1},{4,5},{5,4},{6,7},{7,6},{8,10},{9,11},{10,... | collective-permute-start | bytes 1376264 | tf_op jit(solution)/shard_map/ppermute | solution.py:299
  53.7 48.1 %collective-permute-start = (bf16[256,2048]{1,0:T(8,128)(2,1)}, bf16[256,2048]{1,0:T(8,128)(2,1)S(1)}, u32[]{:S(2)}, u32[]{:S(2)}) collective-permute-start(bf16[256,2048]{1,0:T(8,128)(2,1)} %bitcast.16), channel_id=1, source_target_pairs={{0,4},{4,0},{8,12},{12,8},{16,20},{20,16},{24,28},{28,24},{1,5},{5... | collective-permute-start | bytes 3145736 | tf_op jit(solution)/shard_map/ppermute | solution.py:341
  54.8 20.0 %collective-permute-start.19 = (bf16[896,256]{1,0:T(8,128)(2,1)}, bf16[896,256]{1,0:T(8,128)(2,1)S(1)}, u32[]{:S(2)}, u32[]{:S(2)}) collective-permute-start(bf16[896,256]{1,0:T(8,128)(2,1)} %collective-permute-done.17.refs_3_), channel_id=1, source_target_pairs={{0,2},{1,3},{2,0},{3,1},{4,5},{5,4},{6,7},{7,6},{8,10},{9,11},{10,... | collective-permute-start | bytes 1376264 | tf_op jit(solution)/shard_map/ppermute | solution.py:300
  67.7 17.2 %collective-permute-start.13 = (bf16[512,256]{1,0:T(8,128)(2,1)S(1)}, bf16[512,256]{1,0:T(8,128)(2,1)S(1)}, u32[]{:S(2)}, u32[]{:S(2)}) collective-permute-start(bf16[512,256]{1,0:T(8,128)(2,1)S(1)} %get-tuple-element.18.refs_5_), channel_id=1, source_target_pairs={{0,8},{4,12},{8,16},{12,20},{16,24},{20,28},{1,9},{5,13},{9,17},{1... | collective-permute-start | bytes 786440 | tf_op jit(solution)/shard_map/ppermute | solution.py:380
  69.0 14.6 %collective-permute-start.5 = (bf16[512,256]{1,0:T(8,128)(2,1)S(1)}, bf16[512,256]{1,0:T(8,128)(2,1)S(1)}, u32[]{:S(2)}, u32[]{:S(2)}) collective-permute-start(bf16[512,256]{1,0:T(8,128)(2,1)S(1)} %shard_map.67.refs_0_), channel_id=1, source_target_pairs={{0,8},{4,12},{8,16},{12,20},{16,24},{20,28},{1,9},{5,13},{9,17},{1... | collective-permute-start | bytes 786440 | tf_op jit(solution)/shard_map/ppermute | solution.py:380
  73.3 15.9 %collective-permute-start.25 = (bf16[512,256]{1,0:T(8,128)(2,1)S(1)}, bf16[512,256]{1,0:T(8,128)(2,1)S(1)}, u32[]{:S(2)}, u32[]{:S(2)}) collective-permute-start(bf16[512,256]{1,0:T(8,128)(2,1)S(1)} %get-tuple-element.24.refs_5_), channel_id=1, source_target_pairs={{0,8},{4,12},{8,16},{12,20},{16,24},{20,28},{1,9},{5,13},{9,17},{1... | collective-permute-start | bytes 786440 | tf_op jit(solution)/shard_map/ppermute | solution.py:380
  77.8 17.1 %collective-permute-start.20 = (bf16[512,256]{1,0:T(8,128)(2,1)S(1)}, bf16[512,256]{1,0:T(8,128)(2,1)S(1)}, u32[]{:S(2)}, u32[]{:S(2)}) collective-permute-start(bf16[512,256]{1,0:T(8,128)(2,1)S(1)} %get-tuple-element.22.refs_1_), channel_id=1, source_target_pairs={{0,8},{4,12},{8,16},{12,20},{16,24},{20,28},{1,9},{5,13},{9,17},{1... | collective-permute-start | bytes 786440 | tf_op jit(solution)/shard_map/ppermute | solution.py:380
  83.7 16.9 %collective-permute-start.6 = (bf16[512,256]{1,0:T(8,128)(2,1)S(1)}, bf16[512,256]{1,0:T(8,128)(2,1)S(1)}, u32[]{:S(2)}, u32[]{:S(2)}) collective-permute-start(bf16[512,256]{1,0:T(8,128)(2,1)S(1)} %collective-permute-done.5.refs_1_), channel_id=1, source_target_pairs={{8,16},{12,20},{16,24},{20,28},{9,17},{13,21},{17,25},{21,29},{10,... | collective-permute-start | bytes 786440 | tf_op jit(solution)/shard_map/ppermute | solution.py:380
  85.0 21.2 %collective-permute-start.14 = (bf16[512,256]{1,0:T(8,128)(2,1)S(1)}, bf16[512,256]{1,0:T(8,128)(2,1)S(1)}, u32[]{:S(2)}, u32[]{:S(2)}) collective-permute-start(bf16[512,256]{1,0:T(8,128)(2,1)S(1)} %collective-permute-done.13.refs_6_), channel_id=1, source_target_pairs={{8,16},{12,20},{16,24},{20,28},{9,17},{13,21},{17,25},{21,29},{10,... | collective-permute-start | bytes 786440 | tf_op jit(solution)/shard_map/ppermute | solution.py:380
  89.3 22.5 %collective-permute-start.26 = (bf16[512,256]{1,0:T(8,128)(2,1)S(1)}, bf16[512,256]{1,0:T(8,128)(2,1)S(1)}, u32[]{:S(2)}, u32[]{:S(2)}) collective-permute-start(bf16[512,256]{1,0:T(8,128)(2,1)S(1)} %collective-permute-done.25.refs_6_), channel_id=1, source_target_pairs={{8,16},{12,20},{16,24},{20,28},{9,17},{13,21},{17,25},{21,29},{10,... | collective-permute-start | bytes 786440 | tf_op jit(solution)/shard_map/ppermute | solution.py:380
  94.9 22.5 %collective-permute-start.21 = (bf16[512,256]{1,0:T(8,128)(2,1)S(1)}, bf16[512,256]{1,0:T(8,128)(2,1)S(1)}, u32[]{:S(2)}, u32[]{:S(2)}) collective-permute-start(bf16[512,256]{1,0:T(8,128)(2,1)S(1)} %collective-permute-done.20.refs_2_), channel_id=1, source_target_pairs={{8,16},{12,20},{16,24},{20,28},{9,17},{13,21},{17,25},{21,29},{10,... | collective-permute-start | bytes 786440 | tf_op jit(solution)/shard_map/ppermute | solution.py:380
  100.5 33.5 %collective-permute-start.7 = (bf16[512,256]{1,0:T(8,128)(2,1)S(1)}, bf16[512,256]{1,0:T(8,128)(2,1)S(1)}, u32[]{:S(2)}, u32[]{:S(2)}) collective-permute-start(bf16[512,256]{1,0:T(8,128)(2,1)S(1)} %collective-permute-done.6.refs_2_), channel_id=1, source_target_pairs={{16,24},{20,28},{17,25},{21,29},{18,26},{22,30},{19,27},{23,31}} | collective-permute-start | bytes 786440 | tf_op jit(solution)/shard_map/ppermute | solution.py:380
  106.1 27.9 %collective-permute-start.15 = (bf16[256,256]{1,0:T(8,128)(2,1)S(1)}, bf16[256,256]{1,0:T(8,128)(2,1)S(1)}, u32[]{:S(2)}, u32[]{:S(2)}) collective-permute-start(bf16[256,256]{1,0:T(8,128)(2,1)S(1)} %slice.22), channel_id=1, source_target_pairs={{16,24},{20,28},{17,25},{21,29},{18,26},{22,30},{19,27},{23,31}} | collective-permute-start | bytes 393224 | tf_op jit(solution)/shard_map/ppermute | solution.py:380
  111.8 16.8 %collective-permute-start.28 = (bf16[256,256]{1,0:T(8,128)(2,1)S(1)}, bf16[256,256]{1,0:T(8,128)(2,1)S(1)}, u32[]{:S(2)}, u32[]{:S(2)}) collective-permute-start(bf16[256,256]{1,0:T(8,128)(2,1)S(1)} %slice.24), channel_id=1, source_target_pairs={{16,24},{20,28},{17,25},{21,29},{18,26},{22,30},{19,27},{23,31}} | collective-permute-start | bytes 393224 | tf_op jit(solution)/shard_map/ppermute | solution.py:380
  117.4 14.0 %collective-permute-start.27 = (bf16[256,256]{1,0:T(8,128)(2,1)S(1)}, bf16[256,256]{1,0:T(8,128)(2,1)S(1)}, u32[]{:S(2)}, u32[]{:S(2)}) collective-permute-start(bf16[256,256]{1,0:T(8,128)(2,1)S(1)} %slice.23), channel_id=1, source_target_pairs={{16,24},{20,28},{17,25},{21,29},{18,26},{22,30},{19,27},{23,31}} | collective-permute-start | bytes 393224 | tf_op jit(solution)/shard_map/ppermute | solution.py:380
  (14 other events, 118.4 us)

commit v3 on v2

--- a/solution.py
+++ b/solution.py
@@ -35,6 +35,8 @@
     (VALUE, HD, HD, True),
 )
 SPLIT = (1,)
+
+LATE = (3,)
 
 
 def turn(x, cos, sin):
@@ -106,15 +108,17 @@
                 merged[g, pl.ds(at, size), :] = ref[g, n * size : (n + 1) * size, :]
 
 
-def project_kernel(rope, sources, meta, cosine, sine, *refs):
+def project_kernel(rope, sources, numbers, stage, meta, cosine, sine, *refs):
+    carried, outs = (), refs[-sources:]
+    if stage == "close":
+        carried, refs = refs[:sources], refs[sources:]
     acts = refs[:sources]
     pieces = refs[sources:-sources]
-    outs = refs[-sources:]
-
-    def rows_of(ref):
-        total = None
-        for i, piece in enumerate(pieces):
-            term = jnp.dot(ref[meta[3 + i]], piece[...], preferred_element_type=jnp.float32)
+
+    def rows_of(n):
+        total = carried[n][...] if carried else None
+        for i, piece in zip(numbers, pieces):
+            term = jnp.dot(acts[n][meta[3 + i]], piece[...], preferred_element_type=jnp.float32)
             total = term if total is None else total + term
         return total
 
@@ -124,8 +128,12 @@
             total = turn(total, cosine[stretch, :], sine[stretch, :])
         return total.astype(jnp.bfloat16)
 
+    if stage == "open":
+        for n in range(sources):
+            outs[n][...] = rows_of(n)
+        return
     block = acts[0].shape[1]
-    made = ready(rows_of(acts[0]), 0)
+    made = ready(rows_of(0), 0)
     if sources == 1:
         outs[0][...] = made
         return
@@ -135,7 +143,7 @@
 
     @pl.when(meta[1] > 0)
     def _():
-        outs[1][rows:, :] = ready(rows_of(acts[1]), block)
+        outs[1][rows:, :] = ready(rows_of(1), block)
 
     @pl.when(meta[1] == 0)
     def _():
@@ -143,9 +151,8 @@
 
 
 def cut_kernel(at, meta, weight, out, sem):
-    width = out.shape[1]
     first = pl.multiple_of(meta[0] * HEADS * HD + at, HALF)
-    copy = pltpu.make_async_copy(weight.at[:, pl.ds(first, width)], out, sem)
+    copy = pltpu.make_async_copy(weight.at[:, pl.ds(first, out.shape[1])], out, sem)
     copy.start()
     copy.wait()
 
@@ -362,16 +369,23 @@
     climbed = []
     for i, (kind, at, width, shifted) in enumerate(CHUNKS):
         sources = acts + more if shifted else acts
-        made = call(
-            functools.partial(project_kernel, kind == KEY, len(sources)),
-            [
-                jax.ShapeDtypeStruct((n, width), bf16)
-                for n in ((rows, block) if shifted else (block,))
-            ],
-            (meta, *laid, *sources, *pieces[i]),
-            flops=2 * block * depth * width,
-            limit=12 * MIB,
-        )
+        results = [
+            jax.ShapeDtypeStruct((n, width), bf16)
+            for n in ((rows, block) if shifted else (block,))
+        ]
+        stages = [("whole", tuple(range(len(pieces[i]))))]
+        if i in LATE and relay:
+            stages = [("open", (0, 1, 3)), ("close", (2,))]
+        made = ()
+        for stage, numbers in stages:
+            sums = [jax.ShapeDtypeStruct((x.shape[1], width), f32) for x in sources]
+            made = call(
+                functools.partial(project_kernel, kind == KEY, len(sources), numbers, stage),
+                sums if stage == "open" else results,
+                (meta, *laid, *made, *sources, *[pieces[i][n] for n in numbers]),
+                flops=2 * block * depth * width * len(numbers) // len(pieces[i]),
+                limit=12 * MIB,
+            )
         steps = [made]
         for step in range(1, chips):
             sent = made[-1] if step == 1 else steps[-1]

time: 143 us -> 143 us (level)
    unnamed x16 -> x12, local copies, waits for them, and re-layouts: 3.27 us -> 2.44 us
    pallas_call x10 -> x11, Pallas kernels: 28.2 us -> 28.9 us  [call(): pl.pallas_call(kernel, out_shape=outs, in_specs=[SMEM] * scalars + [VMEM]...]
  transfers between devices with their start and end apart: 30 -> 30, of which waited for: 17 -> 17; matrix products, arithmetic and copies ran while one was open for 3% -> 3% of each run, Pallas kernels for 21% -> 22%
where the time goes in v3:
time: 143 us; the launch traced here: 142 us
  waiting for transfers between devices  64.8 us (45%)
  Pallas kernels  33.9 us (24%)
  starting transfers between devices  33.9 us (24%)
  local copies, waits for them, and re-layouts  5.44 us (4%)
  other arithmetic  2.64 us (2%)
    ppermute x12, waiting for transfers between devices, local(): steps.append(lax.ppermute(sent, 'seq', climb(step)))  35.7 us
    pallas_call x11, Pallas kernels, call(): pl.pallas_call(kernel, out_shape=outs, in_specs=[SMEM] * scalars + [VMEM]...  28.9 us
    ppermute x12, starting transfers between devices, local(): steps.append(lax.ppermute(sent, 'seq', climb(step)))  15.8 us
    ppermute x4, waiting for transfers between devices, local(): near = lax.ppermute(own, both, route((1, 2)))  14.3 us
    ppermute x1, waiting for transfers between devices, local(): risen = lax.ppermute(hidden[0, :lead], 'seq', climb(1))  7.27 us
    ppermute x4, starting transfers between devices, local(): next_ = lax.ppermute(own, both, route((2, 1)))  5.9 us
    ppermute x4, waiting for transfers between devices, local(): far = lax.ppermute(near, both, route((2, 1)))  5.12 us
    ppermute x4, starting transfers between devices, local(): far = lax.ppermute(near, both, route((2, 1)))  4.95 us
  transfers between devices with their start and end apart: 30, of which 17 were waited for; matrix products, arithmetic and copies ran while one was open for 3% of the time, Pallas kernels for 22%

profile of v3, /device:TPU:25, one launch (start us, length us, event | category | flops | bytes accessed | tf_op | source)
XLA Modules:
  0.0 141.8 jit_solution(2104661896337092646)
XLA Ops:
  2.2 3.2 %shard_map.65.own = bf16[4,256,896]{2,1,0:T(8,128)(2,1)} custom-call(f32[1,3584]{1,0:T(1,128)S(1)} %broadcast_in_dim.8.gain, bf16[256,3584]{1,0:T(8,128)(2,1)S(1)} %bitcast.15), custom_call_target="tpu_custom_call" | custom-call | flops 4587520 | bytes 3670016 | tf_op jit(solution)/shard_map/pallas_call | solution.py:314
  14.5 6.1 %collective-permute-done.10.refs_3_ = bf16[896,256]{1,0:T(8,128)(2,1)} collective-permute-done((bf16[896,256]{1,0:T(8,128)(2,1)S(1)}, bf16[896,256]{1,0:T(8,128)(2,1)}, u32[]{:S(2)}, u32[]{:S(2)}) %collective-permute-start.10) | collective-permute-done | bytes 458784 | tf_op jit(solution)/shard_map/ppermute | solution.py:305
  20.6 2.2 %collective-permute-start.3 = (bf16[896,256]{1,0:T(8,128)(2,1)S(1)}, bf16[896,256]{1,0:T(8,128)(2,1)}, u32[]{:S(2)}, u32[]{:S(2)}) collective-permute-start(bf16[896,256]{1,0:T(8,128)(2,1)S(1)} %constant_dynamic-slice_fusion.refs_1_), channel_id=1, source_target_pairs={{0,2},{1,3},{2,0},{3,1},{4,5},{5,4},{6,7},{7,6},{8,10},{9,11},{10,... | collective-permute-start | bytes 1376264 | tf_op jit(solution)/shard_map/ppermute | solution.py:306
  24.0 7.3 %collective-permute-done.8.own = bf16[128,3584]{1,0:T(8,128)(2,1)} collective-permute-done((bf16[128,3584]{1,0:T(8,128)(2,1)}, bf16[128,3584]{1,0:T(8,128)(2,1)}, u32[]{:S(2)}, u32[]{:S(2)}) %collective-permute-start.8) | collective-permute-done | bytes 917536 | tf_op jit(solution)/shard_map/ppermute | solution.py:338
  35.4 1.9 %collective-permute-done.22.refs_3_ = bf16[896,256]{1,0:T(8,128)(2,1)} collective-permute-done((bf16[896,256]{1,0:T(8,128)(2,1)S(1)}, bf16[896,256]{1,0:T(8,128)(2,1)}, u32[]{:S(2)}, u32[]{:S(2)}) %collective-permute-start.22) | collective-permute-done | bytes 458784 | tf_op jit(solution)/shard_map/ppermute | solution.py:305
  38.6 6.2 %collective-permute-done.17.refs_3_ = bf16[896,256]{1,0:T(8,128)(2,1)} collective-permute-done((bf16[896,256]{1,0:T(8,128)(2,1)S(1)}, bf16[896,256]{1,0:T(8,128)(2,1)}, u32[]{:S(2)}, u32[]{:S(2)}) %collective-permute-start.17) | collective-permute-done | bytes 458784 | tf_op jit(solution)/shard_map/ppermute | solution.py:305
  48.3 4.2 %collective-permute-done.23.refs_4_ = bf16[896,256]{1,0:T(8,128)(2,1)S(1)} collective-permute-done((bf16[896,256]{1,0:T(8,128)(2,1)}, bf16[896,256]{1,0:T(8,128)(2,1)S(1)}, u32[]{:S(2)}, u32[]{:S(2)}) %collective-permute-start.23) | collective-permute-done | bytes 458784 | tf_op jit(solution)/shard_map/ppermute | solution.py:307
  57.5 2.4 %shard_map.66.refs_0_.refs_2_ = bf16[4,512,896]{2,1,0:T(8,128)(2,1)S(1)} custom-call(s32[7]{0:T(128)S(1)} %stack.27.meta, bf16[4,256,896]{2,1,0:T(8,128)(2,1)} %shard_map.65.own, bf16[4,256,896]{2,1,0:T(8,128)(2,1)} %collective-permute-done.1.other), custom_call_target="tpu_custom_call" | custom-call | flops 917504 | bytes 3670044 | tf_op jit(solution)/shard_map/pallas_call | solution.py:249
  59.9 2.2 %shard_map.68.refs_1_.refs_3_ = bf16[4,256,896]{2,1,0:T(8,128)(2,1)S(1)} custom-call(s32[7]{0:T(128)S(1)} %stack.27.meta, f32[1,3584]{1,0:T(1,128)S(1)} %broadcast_in_dim.8.gain, bf16[128,3584]{1,0:T(8,128)(2,1)} %collective-permute-done.8.own, bf16[128,3584]{1,0:T(8,128)(2,1)S(1)} %copy-done.5), custom_call_target="tpu_custom_call" | custom-call | flops 4587520 | bytes 1849372 | tf_op jit(solution)/shard_map/pallas_call | solution.py:249
  62.1 2.4 %shard_map.75 = (f32[512,256]{1,0:T(8,128)S(1)}, f32[256,256]{1,0:T(8,128)S(1)}) custom-call(s32[7]{0:T(128)S(1)} %stack.27.meta, f32[768,128]{1,0:T(8,128)S(1)} %get-tuple-element.38.cosine, f32[768,128]{1,0:T(8,128)S(1)} %get-tuple-element.37.sine, bf16[4,512,896]{2,1,0:T(8,128)(2,1)S(1)} %shard_map.66.refs_0_.refs_2_, ...), custom_call_target="tpu_custom_call" | custom-call | flops 704643072 | bytes 7667740 | tf_op jit(solution)/shard_map/pallas_call | solution.py:249
  64.5 3.1 %shard_map.70 = (bf16[256,256]{1,0:T(8,128)(2,1)S(1)}, bf16[512,256]{1,0:T(8,128)(2,1)S(1)}) custom-call(s32[7]{0:T(128)S(1)} %stack.27.meta, f32[768,128]{1,0:T(8,128)S(1)} %get-tuple-element.38.cosine, f32[768,128]{1,0:T(8,128)S(1)} %get-tuple-element.37.sine, bf16[4,512,896]{2,1,0:T(8,128)(2,1)S(1)} %shard_map.66.refs_0_.refs_2_, ...), custom_call_target="tpu_custom_call" | custom-call | flops 939524096 | bytes 8126492 | tf_op jit(solution)/shard_map/pallas_call | solution.py:249
  68.9 2.4 %shard_map.67.refs_0_ = bf16[512,256]{1,0:T(8,128)(2,1)S(1)} custom-call(s32[7]{0:T(128)S(1)} %stack.27.meta, f32[768,128]{1,0:T(8,128)S(1)} %get-tuple-element.38.cosine, f32[768,128]{1,0:T(8,128)S(1)} %get-tuple-element.37.sine, bf16[4,512,896]{2,1,0:T(8,128)(2,1)S(1)} %shard_map.66.refs_0_.refs_2_, ...), custom_call_target="tpu_custom_call" | custom-call | flops 939524096 | bytes 6291484 | tf_op jit(solution)/shard_map/pallas_call | solution.py:249
  75.4 3.0 %shard_map.73 = (bf16[256,256]{1,0:T(8,128)(2,1)S(1)}, bf16[512,256]{1,0:T(8,128)(2,1)S(1)}) custom-call(s32[7]{0:T(128)S(1)} %stack.27.meta, f32[768,128]{1,0:T(8,128)S(1)} %get-tuple-element.38.cosine, f32[768,128]{1,0:T(8,128)S(1)} %get-tuple-element.37.sine, bf16[4,512,896]{2,1,0:T(8,128)(2,1)S(1)} %shard_map.66.refs_0_.refs_2_, ...), custom_call_target="tpu_custom_call" | custom-call | flops 939524096 | bytes 8126492 | tf_op jit(solution)/shard_map/pallas_call | solution.py:249
  79.7 3.9 %collective-permute-done.5.refs_1_ = bf16[512,256]{1,0:T(8,128)(2,1)S(1)} collective-permute-done((bf16[512,256]{1,0:T(8,128)(2,1)S(1)}, bf16[512,256]{1,0:T(8,128)(2,1)S(1)}, u32[]{:S(2)}, u32[]{:S(2)}) %collective-permute-start.5) | collective-permute-done | bytes 262176 | tf_op jit(solution)/shard_map/ppermute | solution.py:394
  86.2 3.0 %collective-permute-done.25.refs_6_ = bf16[512,256]{1,0:T(8,128)(2,1)S(1)} collective-permute-done((bf16[512,256]{1,0:T(8,128)(2,1)S(1)}, bf16[512,256]{1,0:T(8,128)(2,1)S(1)}, u32[]{:S(2)}, u32[]{:S(2)}) %collective-permute-start.25) | collective-permute-done | bytes 262176 | tf_op jit(solution)/shard_map/ppermute | solution.py:394
  90.5 4.3 %collective-permute-done.20.refs_2_ = bf16[512,256]{1,0:T(8,128)(2,1)S(1)} collective-permute-done((bf16[512,256]{1,0:T(8,128)(2,1)S(1)}, bf16[512,256]{1,0:T(8,128)(2,1)S(1)}, u32[]{:S(2)}, u32[]{:S(2)}) %collective-permute-start.20) | collective-permute-done | bytes 262176 | tf_op jit(solution)/shard_map/ppermute | solution.py:394
  96.1 4.3 %collective-permute-done.6.refs_2_ = bf16[512,256]{1,0:T(8,128)(2,1)S(1)} collective-permute-done((bf16[512,256]{1,0:T(8,128)(2,1)S(1)}, bf16[512,256]{1,0:T(8,128)(2,1)S(1)}, u32[]{:S(2)}, u32[]{:S(2)}) %collective-permute-start.6) | collective-permute-done | bytes 262176 | tf_op jit(solution)/shard_map/ppermute | solution.py:394
  102.7 3.4 %collective-permute-done.14.refs_7_ = bf16[512,256]{1,0:T(8,128)(2,1)S(1)} collective-permute-done((bf16[512,256]{1,0:T(8,128)(2,1)S(1)}, bf16[512,256]{1,0:T(8,128)(2,1)S(1)}, u32[]{:S(2)}, u32[]{:S(2)}) %collective-permute-start.14) | collective-permute-done | bytes 262176 | tf_op jit(solution)/shard_map/ppermute | solution.py:394
  107.5 4.1 %collective-permute-done.26.refs_7_ = bf16[512,256]{1,0:T(8,128)(2,1)S(1)} collective-permute-done((bf16[512,256]{1,0:T(8,128)(2,1)S(1)}, bf16[512,256]{1,0:T(8,128)(2,1)S(1)}, u32[]{:S(2)}, u32[]{:S(2)}) %collective-permute-start.26) | collective-permute-done | bytes 262176 | tf_op jit(solution)/shard_map/ppermute | solution.py:394
  113.0 4.3 %collective-permute-done.21.refs_3_ = bf16[512,256]{1,0:T(8,128)(2,1)S(1)} collective-permute-done((bf16[512,256]{1,0:T(8,128)(2,1)S(1)}, bf16[512,256]{1,0:T(8,128)(2,1)S(1)}, u32[]{:S(2)}, u32[]{:S(2)}) %collective-permute-start.21) | collective-permute-done | bytes 262176 | tf_op jit(solution)/shard_map/ppermute | solution.py:394
  118.6 4.4 %shard_map.77 = (f32[2,512,1]{2,1,0:T(8,128)S(1)}, f32[2,512,256]{2,1,0:T(8,128)S(1)}) custom-call(s32[7]{0:T(128)S(1)} %stack.27.meta, bf16[4,512,256]{2,1,0:T(8,128)(2,1)S(1)} %shard_map.64.rotated, bf16[256,256]{1,0:T(8,128)(2,1)S(1)} %get-tuple-element.23.refs_0_, bf16[512,256]{1,0:T(8,128)(2,1)S(1)} %get-tuple-element.24.refs_1_, ...), custom_call_target="tpu_custom_call" | custom-call | flops 1879048192 | bytes 2883612 | tf_op jit(solution)/shard_map/pallas_call | solution.py:249
  123.0 5.5 %collective-permute-done.28.refs_3_ = bf16[256,256]{1,0:T(8,128)(2,1)S(1)} collective-permute-done((bf16[256,256]{1,0:T(8,128)(2,1)S(1)}, bf16[256,256]{1,0:T(8,128)(2,1)S(1)}, u32[]{:S(2)}, u32[]{:S(2)}) %collective-permute-start.28) | collective-permute-done | bytes 131104 | tf_op jit(solution)/shard_map/ppermute | solution.py:394
  128.5 2.8 %collective-permute-done.27.refs_2_ = bf16[256,256]{1,0:T(8,128)(2,1)S(1)} collective-permute-done((bf16[256,256]{1,0:T(8,128)(2,1)S(1)}, bf16[256,256]{1,0:T(8,128)(2,1)S(1)}, u32[]{:S(2)}, u32[]{:S(2)}) %collective-permute-start.27) | collective-permute-done | bytes 131104 | tf_op jit(solution)/shard_map/ppermute | solution.py:394
  133.9 5.2 %shard_map.71 = (bf16[256,512]{1,0:T(8,128)(2,1)S(1)}, bf16[256,512]{1,0:T(8,128)(2,1)S(1)}) custom-call(s32[7]{0:T(128)S(1)} %stack.27.meta, bf16[4,512,256]{2,1,0:T(8,128)(2,1)S(1)} %shard_map.64.rotated, bf16[512,256]{1,0:T(8,128)(2,1)S(1)} %shard_map.67.refs_0_, bf16[512,256]{1,0:T(8,128)(2,1)S(1)} %collective-permute-done.5.refs_1_, ...), custom_call_target="tpu_custom_call" | custom-call | flops 2147483648 | bytes 3145756 | tf_op jit(solution)/shard_map/pallas_call | solution.py:249
  (78 shorter events, 49.0 us)
Async XLA Ops:
  5.5 48.2 %collective-permute-start.1 = (bf16[4,256,896]{2,1,0:T(8,128)(2,1)}, bf16[4,256,896]{2,1,0:T(8,128)(2,1)}, u32[]{:S(2)}, u32[]{:S(2)}) collective-permute-start(bf16[4,256,896]{2,1,0:T(8,128)(2,1)} %shard_map.65.own), channel_id=1, source_target_pairs={{0,4},{4,0},{8,12},{12,8},{16,20},{20,16},{24,28},{28,24},{1,5},{5... | collective-permute-start | bytes 5505032 | tf_op jit(solution)/shard_map/ppermute | solution.py:328
  7.2 24.1 %collective-permute-start.8 = (bf16[128,3584]{1,0:T(8,128)(2,1)}, bf16[128,3584]{1,0:T(8,128)(2,1)}, u32[]{:S(2)}, u32[]{:S(2)}) collective-permute-start(bf16[128,3584]{1,0:T(8,128)(2,1)} %slice_bitcast_fusion), channel_id=1, source_target_pairs={{0,8},{4,12},{8,16},{12,20},{16,24},{20,28},{1,9},{5,13},{9,17},{1... | collective-permute-start | bytes 2752520 | tf_op jit(solution)/shard_map/ppermute | solution.py:338
  13.6 19.2 %collective-permute-start.2 = (bf16[896,256]{1,0:T(8,128)(2,1)S(1)}, bf16[896,256]{1,0:T(8,128)(2,1)}, u32[]{:S(2)}, u32[]{:S(2)}) collective-permute-start(bf16[896,256]{1,0:T(8,128)(2,1)S(1)} %constant_dynamic-slice_fusion.refs_1_), channel_id=1, source_target_pairs={{0,1},{1,0},{2,3},{3,2},{4,6},{5,7},{6,4},{7,5},{8,9},{9,8},{10,11... | collective-permute-start | bytes 1376264 | tf_op jit(solution)/shard_map/ppermute | solution.py:305
  20.6 13.5 %collective-permute-start.3 = (bf16[896,256]{1,0:T(8,128)(2,1)S(1)}, bf16[896,256]{1,0:T(8,128)(2,1)}, u32[]{:S(2)}, u32[]{:S(2)}) collective-permute-start(bf16[896,256]{1,0:T(8,128)(2,1)S(1)} %constant_dynamic-slice_fusion.refs_1_), channel_id=1, source_target_pairs={{0,2},{1,3},{2,0},{3,1},{4,5},{5,4},{6,7},{7,6},{8,10},{9,11},{10,... | collective-permute-start | bytes 1376264 | tf_op jit(solution)/shard_map/ppermute | solution.py:306
  23.8 13.5 %collective-permute-start.22 = (bf16[896,256]{1,0:T(8,128)(2,1)S(1)}, bf16[896,256]{1,0:T(8,128)(2,1)}, u32[]{:S(2)}, u32[]{:S(2)}) collective-permute-start(bf16[896,256]{1,0:T(8,128)(2,1)S(1)} %shard_map.74.refs_2_), channel_id=1, source_target_pairs={{0,1},{1,0},{2,3},{3,2},{4,6},{5,7},{6,4},{7,5},{8,9},{9,8},{10,11... | collective-permute-start | bytes 1376264 | tf_op jit(solution)/shard_map/ppermute | solution.py:305
  31.3 22.6 %collective-permute-start.9 = (bf16[128,3584]{1,0:T(8,128)(2,1)}, bf16[128,3584]{1,0:T(8,128)(2,1)S(1)}, u32[]{:S(2)}, u32[]{:S(2)}) collective-permute-start(bf16[128,3584]{1,0:T(8,128)(2,1)} %collective-permute-done.8.own), channel_id=1, source_target_pairs={{0,4},{4,0},{8,12},{12,8},{16,20},{20,16},{24,28},{28,24},{1,5},{5... | collective-permute-start | bytes 2752520 | tf_op jit(solution)/shard_map/ppermute | solution.py:339
  34.1 12.9 %collective-permute-start.12 = (bf16[896,256]{1,0:T(8,128)(2,1)}, bf16[896,256]{1,0:T(8,128)(2,1)S(1)}, u32[]{:S(2)}, u32[]{:S(2)}) collective-permute-start(bf16[896,256]{1,0:T(8,128)(2,1)} %collective-permute-done.10.refs_3_), channel_id=1, source_target_pairs={{0,2},{1,3},{2,0},{3,1},{4,5},{5,4},{6,7},{7,6},{8,10},{9,11},{10,... | collective-permute-start | bytes 1376264 | tf_op jit(solution)/shard_map/ppermute | solution.py:307
  37.3 15.1 %collective-permute-start.23 = (bf16[896,256]{1,0:T(8,128)(2,1)}, bf16[896,256]{1,0:T(8,128)(2,1)S(1)}, u32[]{:S(2)}, u32[]{:S(2)}) collective-permute-start(bf16[896,256]{1,0:T(8,128)(2,1)} %collective-permute-done.22.refs_3_), channel_id=1, source_target_pairs={{0,2},{1,3},{2,0},{3,1},{4,5},{5,4},{6,7},{7,6},{8,10},{9,11},{10,... | collective-permute-start | bytes 1376264 | tf_op jit(solution)/shard_map/ppermute | solution.py:307
  44.8 22.8 %collective-permute-start.4 = (bf16[896,256]{1,0:T(8,128)(2,1)}, bf16[896,256]{1,0:T(8,128)(2,1)S(1)}, u32[]{:S(2)}, u32[]{:S(2)}) collective-permute-start(bf16[896,256]{1,0:T(8,128)(2,1)} %collective-permute-done.2.refs_2_), channel_id=1, source_target_pairs={{0,2},{1,3},{2,0},{3,1},{4,5},{5,4},{6,7},{7,6},{8,10},{9,11},{10,... | collective-permute-start | bytes 1376264 | tf_op jit(solution)/shard_map/ppermute | solution.py:307
  47.0 24.4 %collective-permute-start.24 = (bf16[896,256]{1,0:T(8,128)(2,1)S(1)}, bf16[896,256]{1,0:T(8,128)(2,1)S(1)}, u32[]{:S(2)}, u32[]{:S(2)}) collective-permute-start(bf16[896,256]{1,0:T(8,128)(2,1)S(1)} %shard_map.74.refs_2_), channel_id=1, source_target_pairs={{0,2},{1,3},{2,0},{3,1},{4,5},{5,4},{6,7},{7,6},{8,10},{9,11},{10,... | collective-permute-start | bytes 1376264 | tf_op jit(solution)/shard_map/ppermute | solution.py:306
  52.4 21.5 %collective-permute-start.18 = (bf16[896,256]{1,0:T(8,128)(2,1)S(1)}, bf16[896,256]{1,0:T(8,128)(2,1)S(1)}, u32[]{:S(2)}, u32[]{:S(2)}) collective-permute-start(bf16[896,256]{1,0:T(8,128)(2,1)S(1)} %shard_map.72.refs_2_), channel_id=1, source_target_pairs={{0,2},{1,3},{2,0},{3,1},{4,5},{5,4},{6,7},{7,6},{8,10},{9,11},{10,... | collective-permute-start | bytes 1376264 | tf_op jit(solution)/shard_map/ppermute | solution.py:306
  53.6 48.1 %collective-permute-start = (bf16[256,2048]{1,0:T(8,128)(2,1)}, bf16[256,2048]{1,0:T(8,128)(2,1)S(1)}, u32[]{:S(2)}, u32[]{:S(2)}) collective-permute-start(bf16[256,2048]{1,0:T(8,128)(2,1)} %bitcast.16), channel_id=1, source_target_pairs={{0,4},{4,0},{8,12},{12,8},{16,20},{20,16},{24,28},{28,24},{1,5},{5... | collective-permute-start | bytes 3145736 | tf_op jit(solution)/shard_map/ppermute | solution.py:348
  54.8 20.6 %collective-permute-start.19 = (bf16[896,256]{1,0:T(8,128)(2,1)}, bf16[896,256]{1,0:T(8,128)(2,1)S(1)}, u32[]{:S(2)}, u32[]{:S(2)}) collective-permute-start(bf16[896,256]{1,0:T(8,128)(2,1)} %collective-permute-done.17.refs_3_), channel_id=1, source_target_pairs={{0,2},{1,3},{2,0},{3,1},{4,5},{5,4},{6,7},{7,6},{8,10},{9,11},{10,... | collective-permute-start | bytes 1376264 | tf_op jit(solution)/shard_map/ppermute | solution.py:307
  67.6 17.2 %collective-permute-start.13 = (bf16[512,256]{1,0:T(8,128)(2,1)S(1)}, bf16[512,256]{1,0:T(8,128)(2,1)S(1)}, u32[]{:S(2)}, u32[]{:S(2)}) collective-permute-start(bf16[512,256]{1,0:T(8,128)(2,1)S(1)} %get-tuple-element.20.refs_5_), channel_id=1, source_target_pairs={{0,8},{4,12},{8,16},{12,20},{16,24},{20,28},{1,9},{5,13},{9,17},{1... | collective-permute-start | bytes 786440 | tf_op jit(solution)/shard_map/ppermute | solution.py:394
  74.0 15.2 %collective-permute-start.25 = (bf16[512,256]{1,0:T(8,128)(2,1)S(1)}, bf16[512,256]{1,0:T(8,128)(2,1)S(1)}, u32[]{:S(2)}, u32[]{:S(2)}) collective-permute-start(bf16[512,256]{1,0:T(8,128)(2,1)S(1)} %get-tuple-element.28.refs_5_), channel_id=1, source_target_pairs={{0,8},{4,12},{8,16},{12,20},{16,24},{20,28},{1,9},{5,13},{9,17},{1... | collective-permute-start | bytes 786440 | tf_op jit(solution)/shard_map/ppermute | solution.py:394
  78.4 16.4 %collective-permute-start.20 = (bf16[512,256]{1,0:T(8,128)(2,1)S(1)}, bf16[512,256]{1,0:T(8,128)(2,1)S(1)}, u32[]{:S(2)}, u32[]{:S(2)}) collective-permute-start(bf16[512,256]{1,0:T(8,128)(2,1)S(1)} %get-tuple-element.24.refs_1_), channel_id=1, source_target_pairs={{0,8},{4,12},{8,16},{12,20},{16,24},{20,28},{1,9},{5,13},{9,17},{1... | collective-permute-start | bytes 786440 | tf_op jit(solution)/shard_map/ppermute | solution.py:394
  83.6 16.9 %collective-permute-start.6 = (bf16[512,256]{1,0:T(8,128)(2,1)S(1)}, bf16[512,256]{1,0:T(8,128)(2,1)S(1)}, u32[]{:S(2)}, u32[]{:S(2)}) collective-permute-start(bf16[512,256]{1,0:T(8,128)(2,1)S(1)} %collective-permute-done.5.refs_1_), channel_id=1, source_target_pairs={{8,16},{12,20},{16,24},{20,28},{9,17},{13,21},{17,25},{21,29},{10,... | collective-permute-start | bytes 786440 | tf_op jit(solution)/shard_map/ppermute | solution.py:394
  84.9 21.2 %collective-permute-start.14 = (bf16[512,256]{1,0:T(8,128)(2,1)S(1)}, bf16[512,256]{1,0:T(8,128)(2,1)S(1)}, u32[]{:S(2)}, u32[]{:S(2)}) collective-permute-start(bf16[512,256]{1,0:T(8,128)(2,1)S(1)} %collective-permute-done.13.refs_6_), channel_id=1, source_target_pairs={{8,16},{12,20},{16,24},{20,28},{9,17},{13,21},{17,25},{21,29},{10,... | collective-permute-start | bytes 786440 | tf_op jit(solution)/shard_map/ppermute | solution.py:394
  89.2 22.5 %collective-permute-start.26 = (bf16[512,256]{1,0:T(8,128)(2,1)S(1)}, bf16[512,256]{1,0:T(8,128)(2,1)S(1)}, u32[]{:S(2)}, u32[]{:S(2)}) collective-permute-start(bf16[512,256]{1,0:T(8,128)(2,1)S(1)} %collective-permute-done.25.refs_6_), channel_id=1, source_target_pairs={{8,16},{12,20},{16,24},{20,28},{9,17},{13,21},{17,25},{21,29},{10,... | collective-permute-start | bytes 786440 | tf_op jit(solution)/shard_map/ppermute | solution.py:394
  94.8 22.5 %collective-permute-start.21 = (bf16[512,256]{1,0:T(8,128)(2,1)S(1)}, bf16[512,256]{1,0:T(8,128)(2,1)S(1)}, u32[]{:S(2)}, u32[]{:S(2)}) collective-permute-start(bf16[512,256]{1,0:T(8,128)(2,1)S(1)} %collective-permute-done.20.refs_2_), channel_id=1, source_target_pairs={{8,16},{12,20},{16,24},{20,28},{9,17},{13,21},{17,25},{21,29},{10,... | collective-permute-start | bytes 786440 | tf_op jit(solution)/shard_map/ppermute | solution.py:394
  100.4 33.5 %collective-permute-start.7 = (bf16[512,256]{1,0:T(8,128)(2,1)S(1)}, bf16[512,256]{1,0:T(8,128)(2,1)S(1)}, u32[]{:S(2)}, u32[]{:S(2)}) collective-permute-start(bf16[512,256]{1,0:T(8,128)(2,1)S(1)} %collective-permute-done.6.refs_2_), channel_id=1, source_target_pairs={{16,24},{20,28},{17,25},{21,29},{18,26},{22,30},{19,27},{23,31}} | collective-permute-start | bytes 786440 | tf_op jit(solution)/shard_map/ppermute | solution.py:394
  106.1 27.9 %collective-permute-start.15 = (bf16[256,256]{1,0:T(8,128)(2,1)S(1)}, bf16[256,256]{1,0:T(8,128)(2,1)S(1)}, u32[]{:S(2)}, u32[]{:S(2)}) collective-permute-start(bf16[256,256]{1,0:T(8,128)(2,1)S(1)} %slice.22), channel_id=1, source_target_pairs={{16,24},{20,28},{17,25},{21,29},{18,26},{22,30},{19,27},{23,31}} | collective-permute-start | bytes 393224 | tf_op jit(solution)/shard_map/ppermute | solution.py:394
  111.7 16.8 %collective-permute-start.28 = (bf16[256,256]{1,0:T(8,128)(2,1)S(1)}, bf16[256,256]{1,0:T(8,128)(2,1)S(1)}, u32[]{:S(2)}, u32[]{:S(2)}) collective-permute-start(bf16[256,256]{1,0:T(8,128)(2,1)S(1)} %slice.24), channel_id=1, source_target_pairs={{16,24},{20,28},{17,25},{21,29},{18,26},{22,30},{19,27},{23,31}} | collective-permute-start | bytes 393224 | tf_op jit(solution)/shard_map/ppermute | solution.py:394
  117.3 14.0 %collective-permute-start.27 = (bf16[256,256]{1,0:T(8,128)(2,1)S(1)}, bf16[256,256]{1,0:T(8,128)(2,1)S(1)}, u32[]{:S(2)}, u32[]{:S(2)}) collective-permute-start(bf16[256,256]{1,0:T(8,128)(2,1)S(1)} %slice.23), channel_id=1, source_target_pairs={{16,24},{20,28},{17,25},{21,29},{18,26},{22,30},{19,27},{23,31}} | collective-permute-start | bytes 393224 | tf_op jit(solution)/shard_map/ppermute | solution.py:394
  (12 other events, 114.9 us)

commit v4 on v3

--- a/solution.py
+++ b/solution.py
@@ -243,6 +243,20 @@
                 safe = jnp.where(valid, total[h, pl.ds(at, half), :], 1.0)
                 result = mixture[h, pl.ds(at, half), :] / safe
                 ref[:, h * HD : (h + 1) * HD] = jnp.where(valid, result, 0.0).astype(jnp.bfloat16)
+
+
+def join_kernel(meta, *refs):
+    parts, out, sems = refs[:-2], refs[-2], refs[-1]
+    wide = parts[0].shape[1]
+    copies = []
+    for n, part in enumerate(parts):
+        place = meta[0] if n < HEADS else 1 - meta[0]
+        at = pl.multiple_of((place * HEADS + n % HEADS) * wide, wide)
+        copies.append(pltpu.make_async_copy(part, out.at[:, pl.ds(at, wide)], sems.at[n]))
+    for copy in copies:
+        copy.start()
+    for copy in copies:
+        copy.wait()
 
 
 def call(kernel, outs, operands, scratch=(), flops=0, transcendentals=0, limit=None, scalars=1):
@@ -452,9 +466,16 @@
             )
         mine.append(state[0])
         theirs.append(lax.ppermute(state[1], "seq", swap))
-    low = [jnp.where(core == 0, a, b) for a, b in zip(mine, theirs)]
-    high = [jnp.where(core == 0, b, a) for a, b in zip(mine, theirs)]
-    return jnp.concatenate(low + high, axis=1)[None]
+    parts = (*mine, *theirs)
+    joined = pl.pallas_call(
+        join_kernel,
+        out_shape=jax.ShapeDtypeStruct((rows, HQ * HD), bf16),
+        in_specs=[SMEM] + [VMEM] * len(parts),
+        out_specs=HBM,
+        scratch_shapes=[pltpu.SemaphoreType.DMA((len(parts),))],
+        compiler_params=pltpu.CompilerParams(vmem_limit_bytes=8 * MIB),
+    )(meta, *parts)
+    return joined[None]
 
 
 def solution(mesh):

time: 143 us -> 142 us (level)
  waiting for transfers between devices: 64.8 us -> 61.3 us
  starting transfers between devices: 33.9 us -> 35.5 us
  local copies, waits for them, and re-layouts: 5.44 us -> 6.9 us
    unnamed x12 -> x24, local copies, waits for them, and re-layouts: 2.44 us -> 4.03 us
    pallas_call x0 -> x1, Pallas kernels: none -> 1.54 us  [local(): pl.pallas_call(join_kernel, out_shape=jax.ShapeDtypeStruct((rows, HQ * HD...]
  transfers between devices with their start and end apart: 30 -> 30, of which waited for: 17 -> 16; matrix products, arithmetic and copies ran while one was open for 3% -> 3% of each run, Pallas kernels for 22% -> 21%
where the time goes in v4:
time: 142 us; the launch traced here: 141 us
  waiting for transfers between devices  61.3 us (43%)
  starting transfers between devices  35.5 us (25%)
  Pallas kernels  35 us (25%)
  local copies, waits for them, and re-layouts  6.9 us (5%)
  other arithmetic  1.46 us (1%)
    ppermute x12, waiting for transfers between devices, local(): steps.append(lax.ppermute(sent, 'seq', climb(step)))  34.3 us
    pallas_call x11, Pallas kernels, call(): pl.pallas_call(kernel, out_shape=outs, in_specs=[SMEM] * scalars + [VMEM]...  28.3 us
    ppermute x12, starting transfers between devices, local(): steps.append(lax.ppermute(sent, 'seq', climb(step)))  15.8 us
    ppermute x4, waiting for transfers between devices, local(): near = lax.ppermute(own, both, route((1, 2)))  15.2 us
    ppermute x1, waiting for transfers between devices, local(): risen = lax.ppermute(hidden[0, :lead], 'seq', climb(1))  5.86 us
    ppermute x4, starting transfers between devices, local(): next_ = lax.ppermute(own, both, route((2, 1)))  5.8 us
    ppermute x4, starting transfers between devices, local(): far = lax.ppermute(near, both, route((2, 1)))  4.84 us
    ppermute x4, waiting for transfers between devices, local(): far = lax.ppermute(near, both, route((2, 1)))  4.3 us
  transfers between devices with their start and end apart: 30, of which 16 were waited for; matrix products, arithmetic and copies ran while one was open for 3% of the time, Pallas kernels for 21%

profile of v4, /device:TPU:25, one launch (start us, length us, event | category | flops | bytes accessed | tf_op | source)
XLA Modules:
  0.0 141.3 jit_solution(9910053464985253619)
XLA Ops:
  2.2 3.2 %shard_map.65.own = bf16[4,256,896]{2,1,0:T(8,128)(2,1)} custom-call(f32[1,3584]{1,0:T(1,128)S(1)} %broadcast_in_dim.8.gain, bf16[256,3584]{1,0:T(8,128)(2,1)S(1)} %bitcast.14), custom_call_target="tpu_custom_call" | custom-call | flops 4587520 | bytes 3670016 | tf_op jit(solution)/shard_map/pallas_call | solution.py:328
  13.3 7.3 %collective-permute-done.21.refs_3_ = bf16[896,256]{1,0:T(8,128)(2,1)S(1)} collective-permute-done((bf16[896,256]{1,0:T(8,128)(2,1)S(1)}, bf16[896,256]{1,0:T(8,128)(2,1)S(1)}, u32[]{:S(2)}, u32[]{:S(2)}) %collective-permute-start.21) | collective-permute-done | bytes 458784 | tf_op jit(solution)/shard_map/ppermute | solution.py:319
  20.6 2.2 %collective-permute-start.17 = (bf16[896,256]{1,0:T(8,128)(2,1)S(1)}, bf16[896,256]{1,0:T(8,128)(2,1)}, u32[]{:S(2)}, u32[]{:S(2)}) collective-permute-start(bf16[896,256]{1,0:T(8,128)(2,1)S(1)} %shard_map.72.refs_2_), channel_id=1, source_target_pairs={{0,2},{1,3},{2,0},{3,1},{4,5},{5,4},{6,7},{7,6},{8,10},{9,11},{10,... | collective-permute-start | bytes 1376264 | tf_op jit(solution)/shard_map/ppermute | solution.py:320
  25.4 5.9 %collective-permute-done.8.own = bf16[128,3584]{1,0:T(8,128)(2,1)} collective-permute-done((bf16[128,3584]{1,0:T(8,128)(2,1)}, bf16[128,3584]{1,0:T(8,128)(2,1)}, u32[]{:S(2)}, u32[]{:S(2)}) %collective-permute-start.8) | collective-permute-done | bytes 917536 | tf_op jit(solution)/shard_map/ppermute | solution.py:352
  35.8 1.6 %collective-permute-done.10.refs_3_ = bf16[896,256]{1,0:T(8,128)(2,1)} collective-permute-done((bf16[896,256]{1,0:T(8,128)(2,1)S(1)}, bf16[896,256]{1,0:T(8,128)(2,1)}, u32[]{:S(2)}, u32[]{:S(2)}) %collective-permute-start.10) | collective-permute-done | bytes 458784 | tf_op jit(solution)/shard_map/ppermute | solution.py:319
  38.6 6.3 %collective-permute-done.2.refs_2_ = bf16[896,256]{1,0:T(8,128)(2,1)} collective-permute-done((bf16[896,256]{1,0:T(8,128)(2,1)S(1)}, bf16[896,256]{1,0:T(8,128)(2,1)}, u32[]{:S(2)}, u32[]{:S(2)}) %collective-permute-start.2) | collective-permute-done | bytes 458784 | tf_op jit(solution)/shard_map/ppermute | solution.py:319
  49.4 3.0 %collective-permute-done.18.refs_5_ = bf16[896,256]{1,0:T(8,128)(2,1)S(1)} collective-permute-done((bf16[896,256]{1,0:T(8,128)(2,1)}, bf16[896,256]{1,0:T(8,128)(2,1)S(1)}, u32[]{:S(2)}, u32[]{:S(2)}) %collective-permute-start.18) | collective-permute-done | bytes 458784 | tf_op jit(solution)/shard_map/ppermute | solution.py:321
  57.5 2.4 %shard_map.66.refs_0_.refs_2_ = bf16[4,512,896]{2,1,0:T(8,128)(2,1)S(1)} custom-call(s32[7]{0:T(128)S(1)} %stack.27.meta, bf16[4,256,896]{2,1,0:T(8,128)(2,1)} %shard_map.65.own, bf16[4,256,896]{2,1,0:T(8,128)(2,1)} %collective-permute-done.1.other), custom_call_target="tpu_custom_call" | custom-call | flops 917504 | bytes 3670044 | tf_op jit(solution)/shard_map/pallas_call | solution.py:263
  59.9 2.3 %shard_map.68.refs_1_.refs_3_ = bf16[4,256,896]{2,1,0:T(8,128)(2,1)S(1)} custom-call(s32[7]{0:T(128)S(1)} %stack.27.meta, f32[1,3584]{1,0:T(1,128)S(1)} %broadcast_in_dim.8.gain, bf16[128,3584]{1,0:T(8,128)(2,1)} %collective-permute-done.8.own, bf16[128,3584]{1,0:T(8,128)(2,1)S(1)} %copy-done.5), custom_call_target="tpu_custom_call" | custom-call | flops 4587520 | bytes 1849372 | tf_op jit(solution)/shard_map/pallas_call | solution.py:263
  62.3 1.9 %shard_map.75 = (f32[512,256]{1,0:T(8,128)S(1)}, f32[256,256]{1,0:T(8,128)S(1)}) custom-call(s32[7]{0:T(128)S(1)} %stack.27.meta, f32[768,128]{1,0:T(8,128)S(1)} %get-tuple-element.34.cosine, f32[768,128]{1,0:T(8,128)S(1)} %get-tuple-element.33.sine, bf16[4,512,896]{2,1,0:T(8,128)(2,1)S(1)} %shard_map.66.refs_0_.refs_2_, ...), custom_call_target="tpu_custom_call" | custom-call | flops 704643072 | bytes 7667740 | tf_op jit(solution)/shard_map/pallas_call | solution.py:263
  65.5 3.1 %shard_map.73 = (bf16[256,256]{1,0:T(8,128)(2,1)S(1)}, bf16[512,256]{1,0:T(8,128)(2,1)S(1)}) custom-call(s32[7]{0:T(128)S(1)} %stack.27.meta, f32[768,128]{1,0:T(8,128)S(1)} %get-tuple-element.34.cosine, f32[768,128]{1,0:T(8,128)S(1)} %get-tuple-element.33.sine, bf16[4,512,896]{2,1,0:T(8,128)(2,1)S(1)} %shard_map.66.refs_0_.refs_2_, ...), custom_call_target="tpu_custom_call" | custom-call | flops 939524096 | bytes 8126492 | tf_op jit(solution)/shard_map/pallas_call | solution.py:263
  71.2 2.3 %shard_map.67.refs_0_ = bf16[512,256]{1,0:T(8,128)(2,1)S(1)} custom-call(s32[7]{0:T(128)S(1)} %stack.27.meta, f32[768,128]{1,0:T(8,128)S(1)} %get-tuple-element.34.cosine, f32[768,128]{1,0:T(8,128)S(1)} %get-tuple-element.33.sine, bf16[4,512,896]{2,1,0:T(8,128)(2,1)S(1)} %shard_map.66.refs_0_.refs_2_, ...), custom_call_target="tpu_custom_call" | custom-call | flops 939524096 | bytes 6291484 | tf_op jit(solution)/shard_map/pallas_call | solution.py:263
  75.0 3.0 %shard_map.70 = (bf16[256,256]{1,0:T(8,128)(2,1)S(1)}, bf16[512,256]{1,0:T(8,128)(2,1)S(1)}) custom-call(s32[7]{0:T(128)S(1)} %stack.27.meta, f32[768,128]{1,0:T(8,128)S(1)} %get-tuple-element.34.cosine, f32[768,128]{1,0:T(8,128)S(1)} %get-tuple-element.33.sine, bf16[4,512,896]{2,1,0:T(8,128)(2,1)S(1)} %shard_map.66.refs_0_.refs_2_, ...), custom_call_target="tpu_custom_call" | custom-call | flops 939524096 | bytes 8126492 | tf_op jit(solution)/shard_map/pallas_call | solution.py:263
  79.2 10.9 %collective-permute-done.5.refs_1_ = bf16[512,256]{1,0:T(8,128)(2,1)S(1)} collective-permute-done((bf16[512,256]{1,0:T(8,128)(2,1)S(1)}, bf16[512,256]{1,0:T(8,128)(2,1)S(1)}, u32[]{:S(2)}, u32[]{:S(2)}) %collective-permute-start.5) | collective-permute-done | bytes 262176 | tf_op jit(solution)/shard_map/ppermute | solution.py:408
  94.1 1.7 %collective-permute-done.13.refs_6_ = bf16[512,256]{1,0:T(8,128)(2,1)S(1)} collective-permute-done((bf16[512,256]{1,0:T(8,128)(2,1)S(1)}, bf16[512,256]{1,0:T(8,128)(2,1)S(1)}, u32[]{:S(2)}, u32[]{:S(2)}) %collective-permute-start.13) | collective-permute-done | bytes 262176 | tf_op jit(solution)/shard_map/ppermute | solution.py:408
  97.1 4.3 %collective-permute-done.6.refs_2_ = bf16[512,256]{1,0:T(8,128)(2,1)S(1)} collective-permute-done((bf16[512,256]{1,0:T(8,128)(2,1)S(1)}, bf16[512,256]{1,0:T(8,128)(2,1)S(1)}, u32[]{:S(2)}, u32[]{:S(2)}) %collective-permute-start.6) | collective-permute-done | bytes 262176 | tf_op jit(solution)/shard_map/ppermute | solution.py:408
  103.8 3.2 %collective-permute-done.25.refs_7_ = bf16[512,256]{1,0:T(8,128)(2,1)S(1)} collective-permute-done((bf16[512,256]{1,0:T(8,128)(2,1)S(1)}, bf16[512,256]{1,0:T(8,128)(2,1)S(1)}, u32[]{:S(2)}, u32[]{:S(2)}) %collective-permute-start.25) | collective-permute-done | bytes 262176 | tf_op jit(solution)/shard_map/ppermute | solution.py:408
  108.3 4.3 %collective-permute-done.20.refs_3_ = bf16[512,256]{1,0:T(8,128)(2,1)S(1)} collective-permute-done((bf16[512,256]{1,0:T(8,128)(2,1)S(1)}, bf16[512,256]{1,0:T(8,128)(2,1)S(1)}, u32[]{:S(2)}, u32[]{:S(2)}) %collective-permute-start.20) | collective-permute-done | bytes 262176 | tf_op jit(solution)/shard_map/ppermute | solution.py:408
  114.0 4.3 %collective-permute-done.14.refs_7_ = bf16[512,256]{1,0:T(8,128)(2,1)S(1)} collective-permute-done((bf16[512,256]{1,0:T(8,128)(2,1)S(1)}, bf16[512,256]{1,0:T(8,128)(2,1)S(1)}, u32[]{:S(2)}, u32[]{:S(2)}) %collective-permute-start.14) | collective-permute-done | bytes 262176 | tf_op jit(solution)/shard_map/ppermute | solution.py:408
  119.6 4.4 %shard_map.77 = (f32[2,512,1]{2,1,0:T(8,128)S(1)}, f32[2,512,256]{2,1,0:T(8,128)S(1)}) custom-call(s32[7]{0:T(128)S(1)} %stack.27.meta, bf16[4,512,256]{2,1,0:T(8,128)(2,1)S(1)} %shard_map.64.rotated, bf16[256,256]{1,0:T(8,128)(2,1)S(1)} %get-tuple-element.22.refs_0_, bf16[512,256]{1,0:T(8,128)(2,1)S(1)} %get-tuple-element.23.refs_1_, ...), custom_call_target="tpu_custom_call" | custom-call | flops 1879048192 | bytes 2883612 | tf_op jit(solution)/shard_map/pallas_call | solution.py:263
  124.0 2.7 %collective-permute-done.27.refs_3_ = bf16[256,256]{1,0:T(8,128)(2,1)S(1)} collective-permute-done((bf16[256,256]{1,0:T(8,128)(2,1)S(1)}, bf16[256,256]{1,0:T(8,128)(2,1)S(1)}, u32[]{:S(2)}, u32[]{:S(2)}) %collective-permute-start.27) | collective-permute-done | bytes 131104 | tf_op jit(solution)/shard_map/ppermute | solution.py:408
  126.7 2.8 %collective-permute-done.26.refs_2_ = bf16[256,256]{1,0:T(8,128)(2,1)S(1)} collective-permute-done((bf16[256,256]{1,0:T(8,128)(2,1)S(1)}, bf16[256,256]{1,0:T(8,128)(2,1)S(1)}, u32[]{:S(2)}, u32[]{:S(2)}) %collective-permute-start.26) | collective-permute-done | bytes 131104 | tf_op jit(solution)/shard_map/ppermute | solution.py:408
  129.5 1.6 %shard_map.78 = (bf16[256,512]{1,0:T(8,128)(2,1)S(1)}, bf16[256,512]{1,0:T(8,128)(2,1)S(1)}) custom-call(s32[7]{0:T(128)S(1)} %stack.27.meta, bf16[4,512,256]{2,1,0:T(8,128)(2,1)S(1)} %shard_map.64.rotated, f32[2,512,1]{2,1,0:T(8,128)S(1)} %get-tuple-element.28.refs_0_, f32[2,512,256]{2,1,0:T(8,128)S(1)} %get-tuple-element.29.refs_1_, ...), custom_call_target="tpu_custom_call" | custom-call | flops 268435456 | bytes 2363420 | tf_op jit(solution)/shard_map/pallas_call | solution.py:263
  132.6 5.2 %shard_map.71 = (bf16[256,512]{1,0:T(8,128)(2,1)S(1)}, bf16[256,512]{1,0:T(8,128)(2,1)S(1)}) custom-call(s32[7]{0:T(128)S(1)} %stack.27.meta, bf16[4,512,256]{2,1,0:T(8,128)(2,1)S(1)} %shard_map.64.rotated, bf16[512,256]{1,0:T(8,128)(2,1)S(1)} %shard_map.67.refs_0_, bf16[512,256]{1,0:T(8,128)(2,1)S(1)} %collective-permute-done.5.refs_1_, ...), custom_call_target="tpu_custom_call" | custom-call | flops 2147483648 | bytes 3145756 | tf_op jit(solution)/shard_map/pallas_call | solution.py:263
  (88 shorter events, 50.1 us)
Async XLA Ops:
  5.5 48.2 %collective-permute-start.1 = (bf16[4,256,896]{2,1,0:T(8,128)(2,1)}, bf16[4,256,896]{2,1,0:T(8,128)(2,1)}, u32[]{:S(2)}, u32[]{:S(2)}) collective-permute-start(bf16[4,256,896]{2,1,0:T(8,128)(2,1)} %shard_map.65.own), channel_id=1, source_target_pairs={{0,4},{4,0},{8,12},{12,8},{16,20},{20,16},{24,28},{28,24},{1,5},{5... | collective-permute-start | bytes 5505032 | tf_op jit(solution)/shard_map/ppermute | solution.py:342
  7.2 24.1 %collective-permute-start.8 = (bf16[128,3584]{1,0:T(8,128)(2,1)}, bf16[128,3584]{1,0:T(8,128)(2,1)}, u32[]{:S(2)}, u32[]{:S(2)}) collective-permute-start(bf16[128,3584]{1,0:T(8,128)(2,1)} %slice_bitcast_fusion), channel_id=1, source_target_pairs={{0,8},{4,12},{8,16},{12,20},{16,24},{20,28},{1,9},{5,13},{9,17},{1... | collective-permute-start | bytes 2752520 | tf_op jit(solution)/shard_map/ppermute | solution.py:352
  13.0 20.2 %collective-permute-start.16 = (bf16[896,256]{1,0:T(8,128)(2,1)S(1)}, bf16[896,256]{1,0:T(8,128)(2,1)}, u32[]{:S(2)}, u32[]{:S(2)}) collective-permute-start(bf16[896,256]{1,0:T(8,128)(2,1)S(1)} %shard_map.72.refs_2_), channel_id=1, source_target_pairs={{0,1},{1,0},{2,3},{3,2},{4,6},{5,7},{6,4},{7,5},{8,9},{9,8},{10,11... | collective-permute-start | bytes 1376264 | tf_op jit(solution)/shard_map/ppermute | solution.py:319
  20.6 13.9 %collective-permute-start.17 = (bf16[896,256]{1,0:T(8,128)(2,1)S(1)}, bf16[896,256]{1,0:T(8,128)(2,1)}, u32[]{:S(2)}, u32[]{:S(2)}) collective-permute-start(bf16[896,256]{1,0:T(8,128)(2,1)S(1)} %shard_map.72.refs_2_), channel_id=1, source_target_pairs={{0,2},{1,3},{2,0},{3,1},{4,5},{5,4},{6,7},{7,6},{8,10},{9,11},{10,... | collective-permute-start | bytes 1376264 | tf_op jit(solution)/shard_map/ppermute | solution.py:320
  24.6 12.7 %collective-permute-start.10 = (bf16[896,256]{1,0:T(8,128)(2,1)S(1)}, bf16[896,256]{1,0:T(8,128)(2,1)}, u32[]{:S(2)}, u32[]{:S(2)}) collective-permute-start(bf16[896,256]{1,0:T(8,128)(2,1)S(1)} %shard_map.69.refs_2_), channel_id=1, source_target_pairs={{0,1},{1,0},{2,3},{3,2},{4,6},{5,7},{6,4},{7,5},{8,9},{9,8},{10,11... | collective-permute-start | bytes 1376264 | tf_op jit(solution)/shard_map/ppermute | solution.py:319
  31.3 22.6 %collective-permute-start.9 = (bf16[128,3584]{1,0:T(8,128)(2,1)}, bf16[128,3584]{1,0:T(8,128)(2,1)S(1)}, u32[]{:S(2)}, u32[]{:S(2)}) collective-permute-start(bf16[128,3584]{1,0:T(8,128)(2,1)} %collective-permute-done.8.own), channel_id=1, source_target_pairs={{0,4},{4,0},{8,12},{12,8},{16,20},{20,16},{24,28},{28,24},{1,5},{5... | collective-permute-start | bytes 2752520 | tf_op jit(solution)/shard_map/ppermute | solution.py:353
  34.5 12.9 %collective-permute-start.22 = (bf16[896,256]{1,0:T(8,128)(2,1)}, bf16[896,256]{1,0:T(8,128)(2,1)S(1)}, u32[]{:S(2)}, u32[]{:S(2)}) collective-permute-start(bf16[896,256]{1,0:T(8,128)(2,1)} %copy-done.8), channel_id=1, source_target_pairs={{0,2},{1,3},{2,0},{3,1},{4,5},{5,4},{6,7},{7,6},{8,10},{9,11},{10,... | collective-permute-start | bytes 1376264 | tf_op jit(solution)/shard_map/ppermute | solution.py:321
  37.3 15.1 %collective-permute-start.18 = (bf16[896,256]{1,0:T(8,128)(2,1)}, bf16[896,256]{1,0:T(8,128)(2,1)S(1)}, u32[]{:S(2)}, u32[]{:S(2)}) collective-permute-start(bf16[896,256]{1,0:T(8,128)(2,1)} %collective-permute-done.16.refs_3_), channel_id=1, source_target_pairs={{0,2},{1,3},{2,0},{3,1},{4,5},{5,4},{6,7},{7,6},{8,10},{9,11},{10,... | collective-permute-start | bytes 1376264 | tf_op jit(solution)/shard_map/ppermute | solution.py:321
  44.9 23.7 %collective-permute-start.3 = (bf16[896,256]{1,0:T(8,128)(2,1)S(1)}, bf16[896,256]{1,0:T(8,128)(2,1)S(1)}, u32[]{:S(2)}, u32[]{:S(2)}) collective-permute-start(bf16[896,256]{1,0:T(8,128)(2,1)S(1)} %constant_dynamic-slice_fusion.refs_1_), channel_id=1, source_target_pairs={{0,2},{1,3},{2,0},{3,1},{4,5},{5,4},{6,7},{7,6},{8,10},{9,11},{10,... | collective-permute-start | bytes 1376264 | tf_op jit(solution)/shard_map/ppermute | solution.py:320
  48.2 21.7 %collective-permute-start.4 = (bf16[896,256]{1,0:T(8,128)(2,1)}, bf16[896,256]{1,0:T(8,128)(2,1)S(1)}, u32[]{:S(2)}, u32[]{:S(2)}) collective-permute-start(bf16[896,256]{1,0:T(8,128)(2,1)} %collective-permute-done.2.refs_2_), channel_id=1, source_target_pairs={{0,2},{1,3},{2,0},{3,1},{4,5},{5,4},{6,7},{7,6},{8,10},{9,11},{10,... | collective-permute-start | bytes 1376264 | tf_op jit(solution)/shard_map/ppermute | solution.py:321
  52.5 21.0 %collective-permute-start.11 = (bf16[896,256]{1,0:T(8,128)(2,1)S(1)}, bf16[896,256]{1,0:T(8,128)(2,1)S(1)}, u32[]{:S(2)}, u32[]{:S(2)}) collective-permute-start(bf16[896,256]{1,0:T(8,128)(2,1)S(1)} %shard_map.69.refs_2_), channel_id=1, source_target_pairs={{0,2},{1,3},{2,0},{3,1},{4,5},{5,4},{6,7},{7,6},{8,10},{9,11},{10,... | collective-permute-start | bytes 1376264 | tf_op jit(solution)/shard_map/ppermute | solution.py:320
  53.7 49.2 %collective-permute-start = (bf16[256,2048]{1,0:T(8,128)(2,1)}, bf16[256,2048]{1,0:T(8,128)(2,1)S(1)}, u32[]{:S(2)}, u32[]{:S(2)}) collective-permute-start(bf16[256,2048]{1,0:T(8,128)(2,1)} %bitcast.15), channel_id=1, source_target_pairs={{0,4},{4,0},{8,12},{12,8},{16,20},{20,16},{24,28},{28,24},{1,5},{5... | collective-permute-start | bytes 3145736 | tf_op jit(solution)/shard_map/ppermute | solution.py:362
  54.8 20.1 %collective-permute-start.12 = (bf16[896,256]{1,0:T(8,128)(2,1)}, bf16[896,256]{1,0:T(8,128)(2,1)S(1)}, u32[]{:S(2)}, u32[]{:S(2)}) collective-permute-start(bf16[896,256]{1,0:T(8,128)(2,1)} %collective-permute-done.10.refs_3_), channel_id=1, source_target_pairs={{0,2},{1,3},{2,0},{3,1},{4,5},{5,4},{6,7},{7,6},{8,10},{9,11},{10,... | collective-permute-start | bytes 1376264 | tf_op jit(solution)/shard_map/ppermute | solution.py:321
  68.6 22.9 %collective-permute-start.24 = (bf16[512,256]{1,0:T(8,128)(2,1)S(1)}, bf16[512,256]{1,0:T(8,128)(2,1)S(1)}, u32[]{:S(2)}, u32[]{:S(2)}) collective-permute-start(bf16[512,256]{1,0:T(8,128)(2,1)S(1)} %get-tuple-element.27.refs_5_), channel_id=1, source_target_pairs={{0,8},{4,12},{8,16},{12,20},{16,24},{20,28},{1,9},{5,13},{9,17},{1... | collective-permute-start | bytes 786440 | tf_op jit(solution)/shard_map/ppermute | solution.py:408
  69.9 22.9 %collective-permute-start.19 = (bf16[512,256]{1,0:T(8,128)(2,1)S(1)}, bf16[512,256]{1,0:T(8,128)(2,1)S(1)}, u32[]{:S(2)}, u32[]{:S(2)}) collective-permute-start(bf16[512,256]{1,0:T(8,128)(2,1)S(1)} %get-tuple-element.23.refs_1_), channel_id=1, source_target_pairs={{0,8},{4,12},{8,16},{12,20},{16,24},{20,28},{1,9},{5,13},{9,17},{1... | collective-permute-start | bytes 786440 | tf_op jit(solution)/shard_map/ppermute | solution.py:408
  73.5 16.7 %collective-permute-start.5 = (bf16[512,256]{1,0:T(8,128)(2,1)S(1)}, bf16[512,256]{1,0:T(8,128)(2,1)S(1)}, u32[]{:S(2)}, u32[]{:S(2)}) collective-permute-start(bf16[512,256]{1,0:T(8,128)(2,1)S(1)} %shard_map.67.refs_0_), channel_id=1, source_target_pairs={{0,8},{4,12},{8,16},{12,20},{16,24},{20,28},{1,9},{5,13},{9,17},{1... | collective-permute-start | bytes 786440 | tf_op jit(solution)/shard_map/ppermute | solution.py:408
  77.9 17.9 %collective-permute-start.13 = (bf16[512,256]{1,0:T(8,128)(2,1)S(1)}, bf16[512,256]{1,0:T(8,128)(2,1)S(1)}, u32[]{:S(2)}, u32[]{:S(2)}) collective-permute-start(bf16[512,256]{1,0:T(8,128)(2,1)S(1)} %get-tuple-element.20.refs_5_), channel_id=1, source_target_pairs={{0,8},{4,12},{8,16},{12,20},{16,24},{20,28},{1,9},{5,13},{9,17},{1... | collective-permute-start | bytes 786440 | tf_op jit(solution)/shard_map/ppermute | solution.py:408
  91.5 15.6 %collective-permute-start.25 = (bf16[512,256]{1,0:T(8,128)(2,1)S(1)}, bf16[512,256]{1,0:T(8,128)(2,1)S(1)}, u32[]{:S(2)}, u32[]{:S(2)}) collective-permute-start(bf16[512,256]{1,0:T(8,128)(2,1)S(1)} %collective-permute-done.24.refs_6_), channel_id=1, source_target_pairs={{8,16},{12,20},{16,24},{20,28},{9,17},{13,21},{17,25},{21,29},{10,... | collective-permute-start | bytes 786440 | tf_op jit(solution)/shard_map/ppermute | solution.py:408
  92.8 19.9 %collective-permute-start.20 = (bf16[512,256]{1,0:T(8,128)(2,1)S(1)}, bf16[512,256]{1,0:T(8,128)(2,1)S(1)}, u32[]{:S(2)}, u32[]{:S(2)}) collective-permute-start(bf16[512,256]{1,0:T(8,128)(2,1)S(1)} %collective-permute-done.19.refs_2_), channel_id=1, source_target_pairs={{8,16},{12,20},{16,24},{20,28},{9,17},{13,21},{17,25},{21,29},{10,... | collective-permute-start | bytes 786440 | tf_op jit(solution)/shard_map/ppermute | solution.py:408
  95.8 22.5 %collective-permute-start.14 = (bf16[512,256]{1,0:T(8,128)(2,1)S(1)}, bf16[512,256]{1,0:T(8,128)(2,1)S(1)}, u32[]{:S(2)}, u32[]{:S(2)}) collective-permute-start(bf16[512,256]{1,0:T(8,128)(2,1)S(1)} %collective-permute-done.13.refs_6_), channel_id=1, source_target_pairs={{8,16},{12,20},{16,24},{20,28},{9,17},{13,21},{17,25},{21,29},{10,... | collective-permute-start | bytes 786440 | tf_op jit(solution)/shard_map/ppermute | solution.py:408
  101.4 31.2 %collective-permute-start.7 = (bf16[512,256]{1,0:T(8,128)(2,1)S(1)}, bf16[512,256]{1,0:T(8,128)(2,1)S(1)}, u32[]{:S(2)}, u32[]{:S(2)}) collective-permute-start(bf16[512,256]{1,0:T(8,128)(2,1)S(1)} %collective-permute-done.6.refs_2_), channel_id=1, source_target_pairs={{16,24},{20,28},{17,25},{21,29},{18,26},{22,30},{19,27},{23,31}} | collective-permute-start | bytes 786440 | tf_op jit(solution)/shard_map/ppermute | solution.py:408
  107.0 19.6 %collective-permute-start.27 = (bf16[256,256]{1,0:T(8,128)(2,1)S(1)}, bf16[256,256]{1,0:T(8,128)(2,1)S(1)}, u32[]{:S(2)}, u32[]{:S(2)}) collective-permute-start(bf16[256,256]{1,0:T(8,128)(2,1)S(1)} %slice.24), channel_id=1, source_target_pairs={{16,24},{20,28},{17,25},{21,29},{18,26},{22,30},{19,27},{23,31}} | collective-permute-start | bytes 393224 | tf_op jit(solution)/shard_map/ppermute | solution.py:408
  112.7 16.8 %collective-permute-start.26 = (bf16[256,256]{1,0:T(8,128)(2,1)S(1)}, bf16[256,256]{1,0:T(8,128)(2,1)S(1)}, u32[]{:S(2)}, u32[]{:S(2)}) collective-permute-start(bf16[256,256]{1,0:T(8,128)(2,1)S(1)} %slice.23), channel_id=1, source_target_pairs={{16,24},{20,28},{17,25},{21,29},{18,26},{22,30},{19,27},{23,31}} | collective-permute-start | bytes 393224 | tf_op jit(solution)/shard_map/ppermute | solution.py:408
  118.3 14.3 %collective-permute-start.15 = (bf16[256,256]{1,0:T(8,128)(2,1)S(1)}, bf16[256,256]{1,0:T(8,128)(2,1)S(1)}, u32[]{:S(2)}, u32[]{:S(2)}) collective-permute-start(bf16[256,256]{1,0:T(8,128)(2,1)S(1)} %slice.22), channel_id=1, source_target_pairs={{16,24},{20,28},{17,25},{21,29},{18,26},{22,30},{19,27},{23,31}} | collective-permute-start | bytes 393224 | tf_op jit(solution)/shard_map/ppermute | solution.py:408
  (18 other events, 109.6 us)
